TPU v7x, 256 devices: a whole 4x4x8 slice. The times are simulated.
256 devices in a mesh: blk: 32 (over z, x), span: 8 (over y, core).
Axes of the slice: x: 4, y: 4, z: 8, core: 2. Of those that a mesh axis runs over, the one named last changes fastest.
Arguments:
- fluid_adjoint_in: float32 [5, 256, 256, 128], P(None, 'blk', 'span'), may hold values from -4 to 4
- fluid_source: float32 [5, 256, 256, 128], P(None, 'blk', 'span'), may hold values from -24 to 24
- velocity: float32 [3, 256, 256, 128], P(None, 'blk', 'span'), may hold values from 0.1 to 1
- diffusion: float32 [5], replicated, may hold values from 0.5 to 2
- jacobian: float32 [5, 5], replicated, may hold values from -0.4 to 0.4
- wall_coefficient: float32 [32, 256, 128], P('blk', 'span'), may hold values from 0.5 to 2
- metal_costate_prior: float32 [512, 256, 128], P('blk', 'span'), may hold values from -4 to 4
- solid_source: float32 [512, 256, 128], P('blk', 'span'), may hold values from -12 to 12
- conductivity: float32 [512, 256, 128], P('blk', 'span'), may hold values from 0.3 to 3
- tile_owner: int32 [8, 1024, 1], P('span', 'blk'), may hold values from 0 to 31; in each aligned block of 32 rows (0 to 31, 32 to 63, ..., all dimensions but the last counted through in order) at most 3 rows name the same one
- tile_target: int32 [8, 1024], P('span', 'blk'), may hold values from 0 to 31
Outputs:
- fluid_adjoint: float32 [5, 256, 256, 128], P(None, 'blk', 'span')
- solid_adjoint: float32 [512, 256, 128], P('blk', 'span')
- residual_norms: float32 [6], replicated
Inputs may be any that keep to these rules, and one draw needn't show every extreme that they name: `tile_owner`: within the 32 wall tiles of one fluid block (the rows of one device), no owner is named more than 3 times, a bound that some block reaches; every owner is named by some tile.
All inputs are finite; a program needn't handle non-finite values.
Results may differ from a plain program's by a relative error of at most 0.004.
Values sent between devices are 32-bit elements; how exact they have to be, the bound alone decides.
A program may use at most 64 MiB of HBM per device.

v0:
```python
import jax
import jax.numpy as jnp
from jax import lax
from jax.sharding import PartitionSpec as P

FSWEEPS = 4
SSWEEPS = 4


damping_weight = 0.8


def padded(block, sides, width):
    for axis, dim in sides:
        count = lax.axis_size(axis)
        forward = [(i, i + 1) for i in range(count - 1)]
        backward = [(target, source) for source, target in forward]
        low = lax.ppermute(
            lax.slice_in_dim(block, block.shape[dim] - width, None, axis=dim), axis, forward
        )
        high = lax.ppermute(lax.slice_in_dim(block, 0, width, axis=dim), axis, backward)
        block = jnp.concatenate([low, block, high], axis=dim)
    return block


def fluid_operator(bordered_grid_data, velocity, spread, jacobian):
    centre = bordered_grid_data[:, 1:-1, 1:-1, 1:-1]
    x_next = bordered_grid_data[:, 2:, 1:-1, 1:-1]
    y_next = bordered_grid_data[:, 1:-1, 2:, 1:-1]
    z_next = bordered_grid_data[:, 1:-1, 1:-1, 2:]
    beside_all = (
        x_next
        + bordered_grid_data[:, :-2, 1:-1, 1:-1]
        + y_next
        + bordered_grid_data[:, 1:-1, :-2, 1:-1]
        + z_next
        + bordered_grid_data[:, 1:-1, 1:-1, :-2]
    )
    mixing = jnp.einsum("fg,gxyz->fxyz", jacobian, centre, precision=lax.Precision.HIGHEST)
    velocity_sum = velocity[0] + velocity[1] + velocity[2]
    return (
        (6.0 * spread + velocity_sum) * centre
        - spread * beside_all
        - velocity[0] * x_next
        - velocity[1] * y_next
        - velocity[2] * z_next
        + mixing
    )


def face_conductance(kappa_rim):
    centre = kappa_rim[1:-1, 1:-1, 1:-1]
    return (
        0.5 * (centre + kappa_rim[2:, 1:-1, 1:-1]),
        0.5 * (centre + kappa_rim[:-2, 1:-1, 1:-1]),
        0.5 * (centre + kappa_rim[1:-1, 2:, 1:-1]),
        0.5 * (centre + kappa_rim[1:-1, :-2, 1:-1]),
        0.5 * (centre + kappa_rim[1:-1, 1:-1, 2:]),
        0.5 * (centre + kappa_rim[1:-1, 1:-1, :-2]),
    )


def solid_operator(bordered_grid_data, faces, diagonal):
    centre = bordered_grid_data[1:-1, 1:-1, 1:-1]
    flows = (
        faces[0] * bordered_grid_data[2:, 1:-1, 1:-1]
        + faces[1] * bordered_grid_data[:-2, 1:-1, 1:-1]
    )
    flows = (
        flows
        + faces[2] * bordered_grid_data[1:-1, 2:, 1:-1]
        + faces[3] * bordered_grid_data[1:-1, :-2, 1:-1]
    )
    flows = (
        flows
        + faces[4] * bordered_grid_data[1:-1, 1:-1, 2:]
        + faces[5] * bordered_grid_data[1:-1, 1:-1, :-2]
    )
    return diagonal * centre - flows


def pad_depth(array):
    widths = [(0, 0)] * (array.ndim - 1) + [(1, 1)]
    return jnp.pad(array, widths)


def shards(
    fluid_adjoint_in,
    fluid_source,
    velocity,
    diffusion,
    jacobian,
    wall_coefficient,
    metal_costate_prior,
    solid_source,
    conductivity,
    tile_owner,
    tile_target,
):
    highest = lax.Precision.HIGHEST
    spread = diffusion[:, None, None, None]
    fluid_diagonal = (
        6.0 * spread
        + (velocity[0] + velocity[1] + velocity[2])
        + jnp.diagonal(jacobian)[:, None, None, None]
    )
    adjoint = fluid_adjoint_in
    for iteration in range(FSWEEPS):
        bordered_grid_data = padded(adjoint, (("blk", 1), ("span", 2)), 1)
        bordered_grid_data = pad_depth(bordered_grid_data)
        fluid_residual = fluid_source - fluid_operator(
            bordered_grid_data, velocity, spread, jacobian
        )
        adjoint = adjoint + damping_weight * fluid_residual / fluid_diagonal
    fluid_squares = jnp.sum(fluid_residual * fluid_residual, axis=(1, 2, 3))
    wall_flux = wall_coefficient[0] * adjoint[4, 0]
    rows = wall_flux.shape[0]
    blocks = lax.axis_size("blk")
    myself = lax.axis_index("blk")
    owner_local = tile_owner[0, :, 0]
    target_local = tile_target[0, :]
    owners_all, targets_all = (
        lax.all_gather(owner_local, "blk", axis=0, tiled=True),
        lax.all_gather(target_local, "blk", axis=0, tiled=True),
    )
    owner_grid = owners_all.reshape(blocks, rows)
    target_grid = targets_all.reshape(blocks, rows)
    to_myself = owner_grid == myself
    target_hot = target_grid[:, :, None] == jnp.arange(rows, dtype=jnp.int32)[None, None, :]
    placing = (target_hot & to_myself[:, :, None]).astype(jnp.float32).reshape(blocks * rows, rows)
    arrived = lax.all_gather(wall_flux, "blk", axis=0, tiled=True)
    surface = jnp.dot(placing.T, arrived, precision=highest)
    heat_source = solid_source.at[-1].add(surface)
    thermal_state_grid = metal_costate_prior
    kappa_rim = padded(conductivity, (("blk", 0), ("span", 1)), 1)
    kappa_rim = pad_depth(kappa_rim)
    faces = face_conductance(kappa_rim)
    metal_pivot_entries = faces[0] + faces[1] + faces[2] + faces[3] + faces[4] + faces[5]
    for iteration in range(SSWEEPS):
        bordered_grid_data = padded(thermal_state_grid, (("blk", 0), ("span", 1)), 1)
        bordered_grid_data = pad_depth(bordered_grid_data)
        metal_imbalance_grid = heat_source - solid_operator(
            bordered_grid_data, faces, metal_pivot_entries
        )
        thermal_state_grid = (
            thermal_state_grid + damping_weight * metal_imbalance_grid / metal_pivot_entries
        )
    interface_heat_level = thermal_state_grid[-1]
    boundary_patches_finished = lax.all_gather(interface_heat_level, "blk", axis=0, tiled=True)
    output_entries = jnp.take(boundary_patches_finished, owner_local * rows + target_local, axis=0)
    gas_outcome = adjoint.at[4, 0].add(wall_coefficient[0] * output_entries)
    solid_squares = jnp.sum(metal_imbalance_grid * metal_imbalance_grid)[None]
    totals = lax.psum(jnp.concatenate([fluid_squares, solid_squares]), ("blk", "span"))
    every_processor = lax.axis_size("blk") * lax.axis_size("span")
    fluid_cells = float(adjoint.shape[1] * adjoint.shape[2] * adjoint.shape[3] * every_processor)
    solid_cells = float(
        thermal_state_grid.shape[0]
        * thermal_state_grid.shape[1]
        * thermal_state_grid.shape[2]
        * every_processor
    )
    counts = jnp.array([fluid_cells] * 5 + [solid_cells], jnp.float32)
    magnitude_list = jnp.sqrt(totals / counts)
    return (gas_outcome, thermal_state_grid, magnitude_list)


def solution(mesh):
    placed = (
        P(None, "blk", "span", None),
        P(None, "blk", "span", None),
        P(None, "blk", "span", None),
        P(),
        P(),
        P("blk", "span", None),
        P("blk", "span", None),
        P("blk", "span", None),
        P("blk", "span", None),
        P("span", "blk", None),
        P("span", "blk"),
    )
    return jax.shard_map(
        shards,
        mesh=mesh,
        in_specs=placed,
        out_specs=(P(None, "blk", "span", None), P("blk", "span", None), P()),
        check_vma=False,
    )
```

profile of v0, /device:TPU:2, one launch (start us, length us, event | category | flops | bytes accessed | tf_op | source)
XLA Modules:
  0.0 370.5 jit_solution(5415000750408817278)
XLA Ops:
  0.7 1.6 copy.36
  3.0 3.4 collective-permute-start.1
  6.4 2.4 collective-permute-start
  9.6 3.4 collective-permute-start.17
  13.0 2.4 collective-permute-start.16
  15.5 3.4 collective-permute-start.21
  20.5 26.2 %all-reduce.11 = (s32[1024]{0:T(1024)S(1)}, s32[1024]{0:T(1024)S(1)}) all-reduce(s32[1024]{0:T(1024)S(1)} %bitcast_dynamic-update-slice_fusion.1, s32[1024]{0:T(1024)S(1)} %bitcast_dynamic-update-slice_fusion), channel_id=2, replica_groups=mesh['blk'=32,'span'=8] {'blk'}, use_global_device_ids=true, to_apply=%add.9 | all-reduce | flops 2048 | bytes 16384
  47.4 2.5 collective-permute-start.20
  50.5 1.3 collective-permute-start.2
  51.8 3.0 collective-permute-start.3
  54.8 1.3 collective-permute-start.18
  56.2 3.7 %collective-permute-start.19 = (f32[18,1,128]{2,1,0:T(1,128)S(1)}, f32[18,1,128]{2,1,0:T(1,128)S(1)}, u32[]{:S(2)}, u32[]{:S(2)}) collective-permute-start(f32[18,1,128]{2,1,0:T(1,128)S(1)} %get-tuple-element.70), channel_id=1, source_target_pairs={{0,1},{1,2},{2,3},{3,4},{4,5},{5,6},{6,7},{8,9},{9,10},{10,11},{11... | collective-permute-start | bytes 27656 | tf_op jit(solution)/shard_map/ppermute | solution.py:18
  60.7 2.7 fusion.10
  63.4 1.9 collective-permute-start.4
  65.4 3.9 %collective-permute-start.5 = (f32[5,1,32,128]{3,0,2,1:T(8,128)S(1)}, f32[5,1,32,128]{3,0,2,1:T(8,128)S(1)}, u32[]{:S(2)}, u32[]{:S(2)}) collective-permute-start(f32[5,1,32,128]{3,0,2,1:T(8,128)S(1)} %get-tuple-element.56), channel_id=1, source_target_pairs={{0,8},{8,16},{16,24},{24,32},{32,40},{40,48},{48,56},{56,64},{64,7... | collective-permute-start | bytes 245768 | tf_op jit(solution)/shard_map/ppermute | solution.py:18
  69.3 1.7 collective-permute-done.4
  71.0 1.9 collective-permute-done.5
  72.9 1.3 collective-permute-start.6
  74.2 3.1 collective-permute-start.7
  77.3 0.8 collective-permute-done.7
  78.2 0.8 select_maximum_fusion.8
  79.0 2.2 fusion.11
  81.2 1.9 collective-permute-start.8
  83.1 4.2 %collective-permute-start.9 = (f32[5,1,32,128]{3,0,2,1:T(8,128)S(1)}, f32[5,1,32,128]{3,0,2,1:T(8,128)S(1)}, u32[]{:S(2)}, u32[]{:S(2)}) collective-permute-start(f32[5,1,32,128]{3,0,2,1:T(8,128)S(1)} %get-tuple-element.54), channel_id=1, source_target_pairs={{0,8},{8,16},{16,24},{24,32},{32,40},{40,48},{48,56},{56,64},{64,7... | collective-permute-start | bytes 245768 | tf_op jit(solution)/shard_map/ppermute | solution.py:18
  87.3 1.4 collective-permute-done.8
  88.7 1.8 collective-permute-done.9
  90.5 1.3 collective-permute-start.10
  91.8 3.3 collective-permute-start.11
  95.2 1.3 collective-permute-start.22
  96.5 5.7 %collective-permute-start.23 = (f32[18,1,128]{2,1,0:T(1,128)S(1)}, f32[18,1,128]{2,1,0:T(1,128)S(1)}, u32[]{:S(2)}, u32[]{:S(2)}) collective-permute-start(f32[18,1,128]{2,1,0:T(1,128)S(1)} %get-tuple-element.72), channel_id=1, source_target_pairs={{0,1},{1,2},{2,3},{3,4},{4,5},{5,6},{6,7},{8,9},{9,10},{10,11},{11... | collective-permute-start | bytes 27656 | tf_op jit(solution)/shard_map/ppermute | solution.py:18
  102.2 0.8 select_maximum_fusion.4
  103.0 2.2 fusion.12
  105.2 1.9 collective-permute-start.12
  107.2 3.9 %collective-permute-start.13 = (f32[5,1,32,128]{3,0,2,1:T(8,128)S(1)}, f32[5,1,32,128]{3,0,2,1:T(8,128)S(1)}, u32[]{:S(2)}, u32[]{:S(2)}) collective-permute-start(f32[5,1,32,128]{3,0,2,1:T(8,128)S(1)} %get-tuple-element.52), channel_id=1, source_target_pairs={{0,8},{8,16},{16,24},{24,32},{32,40},{40,48},{48,56},{56,64},{64,7... | collective-permute-start | bytes 245768 | tf_op jit(solution)/shard_map/ppermute | solution.py:18
  111.4 1.0 collective-permute-done.12
  112.4 2.3 collective-permute-done.13
  114.7 1.4 collective-permute-start.14
  116.2 3.1 collective-permute-start.15
  120.1 0.8 select_maximum_fusion
  121.0 2.5 multiply_reduce_fusion
  123.5 59.1 %all_gather.14 = f32[1024,128]{1,0:T(8,128)S(1)} all-gather(f32[32,128]{1,0:T(8,128)S(1)} %bitcast_multiply_fusion), channel_id=1, replica_groups=mesh['blk'=32,'span'=8] {'blk'}, dimensions={0}, use_global_device_ids=true | all-gather | bytes 540672 | tf_op jit(solution)/shard_map/all_gather | solution.py:131
  182.6 0.9 fusion.6
  184.0 1.9 collective-permute-start.24
  186.0 3.9 %collective-permute-start.25 = (f32[1,32,128]{2,1,0:T(8,128)S(1)}, f32[1,32,128]{2,1,0:T(8,128)S(1)}, u32[]{:S(2)}, u32[]{:S(2)}) collective-permute-start(f32[1,32,128]{2,1,0:T(8,128)S(1)} %get-tuple-element.78), channel_id=1, source_target_pairs={{0,8},{8,16},{16,24},{24,32},{32,40},{40,48},{48,56},{56,64},{64,7... | collective-permute-start | bytes 49160 | tf_op jit(solution)/shard_map/ppermute | solution.py:18
  189.9 1.7 collective-permute-done.25
  191.6 1.3 collective-permute-start.26
  192.9 3.0 collective-permute-start.27
  196.0 0.8 collective-permute-done.27
  197.5 1.9 collective-permute-start.28
  199.4 3.9 %collective-permute-start.29 = (f32[1,32,128]{2,1,0:T(8,128)S(1)}, f32[1,32,128]{2,1,0:T(8,128)S(1)}, u32[]{:S(2)}, u32[]{:S(2)}) collective-permute-start(f32[1,32,128]{2,1,0:T(8,128)S(1)} %get-tuple-element.76), channel_id=1, source_target_pairs={{0,8},{8,16},{16,24},{24,32},{32,40},{40,48},{48,56},{56,64},{64,7... | collective-permute-start | bytes 49160 | tf_op jit(solution)/shard_map/ppermute | solution.py:18
  203.4 1.7 collective-permute-done.29
  205.1 1.3 collective-permute-start.30
  206.4 5.1 %collective-permute-start.31 = (f32[18,1,128]{2,1,0:T(1,128)S(1)}, f32[18,1,128]{2,1,0:T(1,128)S(1)}, u32[]{:S(2)}, u32[]{:S(2)}) collective-permute-start(f32[18,1,128]{2,1,0:T(1,128)S(1)} %get-tuple-element.66), channel_id=1, source_target_pairs={{0,1},{1,2},{2,3},{3,4},{4,5},{5,6},{6,7},{8,9},{9,10},{10,11},{11... | collective-permute-start | bytes 27656 | tf_op jit(solution)/shard_map/ppermute | solution.py:18
  211.5 0.8 collective-permute-done.31
  213.1 1.9 collective-permute-start.32
  215.0 4.2 %collective-permute-start.33 = (f32[1,32,128]{2,1,0:T(8,128)S(1)}, f32[1,32,128]{2,1,0:T(8,128)S(1)}, u32[]{:S(2)}, u32[]{:S(2)}) collective-permute-start(f32[1,32,128]{2,1,0:T(8,128)S(1)} %get-tuple-element.74), channel_id=1, source_target_pairs={{0,8},{8,16},{16,24},{24,32},{32,40},{40,48},{48,56},{56,64},{64,7... | collective-permute-start | bytes 49160 | tf_op jit(solution)/shard_map/ppermute | solution.py:18
  219.3 1.4 collective-permute-done.33
  220.7 1.3 collective-permute-start.34
  222.0 4.8 %collective-permute-start.35 = (f32[18,1,128]{2,1,0:T(1,128)S(1)}, f32[18,1,128]{2,1,0:T(1,128)S(1)}, u32[]{:S(2)}, u32[]{:S(2)}) collective-permute-start(f32[18,1,128]{2,1,0:T(1,128)S(1)} %get-tuple-element.64), channel_id=1, source_target_pairs={{0,1},{1,2},{2,3},{3,4},{4,5},{5,6},{6,7},{8,9},{9,10},{10,11},{11... | collective-permute-start | bytes 27656 | tf_op jit(solution)/shard_map/ppermute | solution.py:18
  226.8 0.8 collective-permute-done.35
  227.9 1.0 multiply_reduce_fusion.1
  229.6 89.1 %psum.7 = f32[6]{0:T(128)S(1)} all-reduce(f32[6]{0:T(128)S(1)} %pad_maximum_fusion.78), channel_id=1, replica_groups=mesh['blk'=32,'span'=8] {'blk','span'}, use_global_device_ids=true, to_apply=%region_2.3 | all-reduce | flops 6 | bytes 48 | tf_op jit(solution)/shard_map/psum | solution.py:153
  318.9 49.3 %all-gather.2 = f32[1,1024,128]{2,1,0:T(8,128)S(1)} all-gather(f32[1,32,128]{2,1,0:T(8,128)S(1)} %slice.616), channel_id=4, replica_groups=mesh['blk'=32,'span'=8] {'blk'}, dimensions={1}, use_global_device_ids=true | all-gather | bytes 540672 | tf_op jit(solution)/shard_map/all_gather | solution.py:149
  369.0 1.0 copy.40
  (121 shorter events, 10.3 us)
Async XLA Ops:
  0.6 46.1 %copy-start = (f32[5,5]{1,0:T(8,128)S(1)}, f32[5,5]{1,0:T(8,128)}, u32[]{:S(2)}) copy-start(f32[5,5]{1,0:T(8,128)} %param.20) | copy-start | bytes 304
  0.6 18.4 %copy-start.18 = (u32[256]{0:T(256)S(1)}, u32[256]{0:T(256)}, u32[]{:S(2)}) copy-start(u32[256]{0:T(256)} %constant.146) | copy-start | bytes 3076
  0.7 49.3 %copy-start.3 = (f32[5,8,32,128]{3,2,1,0:T(8,128)S(1)}, f32[5,8,32,128]{3,2,1,0:T(8,128)}, u32[]{:S(2)}) copy-start(f32[5,8,32,128]{3,2,1,0:T(8,128)} %param.16) | copy-start | bytes 1966084
  0.7 18.2 %copy-start.5 = (f32[3,8,32,128]{3,2,1,0:T(8,128)S(1)}, f32[3,8,32,128]{3,2,1,0:T(8,128)}, u32[]{:S(2)}) copy-start(f32[3,8,32,128]{3,2,1,0:T(8,128)} %param.18) | copy-start | bytes 1179652
  0.7 18.3 %copy-start.15 = (f32[5]{0:T(128)S(1)}, f32[5]{0:T(128)}, u32[]{:S(2)}) copy-start(f32[5]{0:T(128)} %param.19) | copy-start | bytes 64
  0.7 14.8 %copy-start.4 = (f32[16,32,128]{2,1,0:T(8,128)S(1)}, f32[16,32,128]{2,1,0:T(8,128)}, u32[]{:S(2)}) copy-start(f32[16,32,128]{2,1,0:T(8,128)} %param.22) | copy-start | bytes 786436
  0.7 49.2 %copy-start.1 = (f32[16,32,128]{2,1,0:T(8,128)S(1)}, f32[16,32,128]{2,1,0:T(8,128)}, u32[]{:S(2)}) copy-start(f32[16,32,128]{2,1,0:T(8,128)} %param.24) | copy-start | bytes 786436
  0.7 19.6 %copy-start.17 = (s32[1,32,1]{1,2,0:T(1,128)S(1)}, s32[1,32,1]{1,2,0:T(1,128)}, u32[]{:S(2)}) copy-start(s32[1,32,1]{1,2,0:T(1,128)} %param.25) | copy-start | bytes 388
  0.7 19.7 %copy-start.16 = (s32[1,32]{1,0:T(1,128)S(1)}, s32[1,32]{1,0:T(1,128)}, u32[]{:S(2)}) copy-start(s32[1,32]{1,0:T(1,128)} %param.26) | copy-start | bytes 388
  3.0 46.9 %collective-permute-start.1 = (f32[5,1,32,128]{3,0,2,1:T(8,128)}, f32[5,1,32,128]{3,0,2,1:T(8,128)S(1)}, u32[]{:S(2)}, u32[]{:S(2)}) collective-permute-start(f32[5,1,32,128]{3,0,2,1:T(8,128)} %get-tuple-element.59), channel_id=1, source_target_pairs={{0,8},{8,16},{16,24},{24,32},{32,40},{40,48},{48,56},{56,64},{64,7... | collective-permute-start | bytes 245768 | tf_op jit(solution)/shard_map/ppermute | solution.py:18
  6.4 44.0 %collective-permute-start = (f32[5,1,32,128]{3,0,2,1:T(8,128)}, f32[5,1,32,128]{3,0,2,1:T(8,128)S(1)}, u32[]{:S(2)}, u32[]{:S(2)}) collective-permute-start(f32[5,1,32,128]{3,0,2,1:T(8,128)} %get-tuple-element.58), channel_id=1, source_target_pairs={{8,0},{16,8},{24,16},{32,24},{40,32},{48,40},{56,48},{64,56},{72,6... | collective-permute-start | bytes 245768 | tf_op jit(solution)/shard_map/ppermute | solution.py:21
  9.6 37.7 %collective-permute-start.17 = (f32[1,32,128]{2,1,0:T(8,128)S(1)}, f32[1,32,128]{2,1,0:T(8,128)S(1)}, u32[]{:S(2)}, u32[]{:S(2)}) collective-permute-start(f32[1,32,128]{2,1,0:T(8,128)S(1)} %get-tuple-element.80), channel_id=1, source_target_pairs={{0,8},{8,16},{16,24},{24,32},{32,40},{40,48},{48,56},{56,64},{64,7... | collective-permute-start | bytes 49160 | tf_op jit(solution)/shard_map/ppermute | solution.py:18
  13.0 36.9 %collective-permute-start.16 = (f32[1,32,128]{2,1,0:T(8,128)S(1)}, f32[1,32,128]{2,1,0:T(8,128)S(1)}, u32[]{:S(2)}, u32[]{:S(2)}) collective-permute-start(f32[1,32,128]{2,1,0:T(8,128)S(1)} %get-tuple-element.81), channel_id=1, source_target_pairs={{8,0},{16,8},{24,16},{32,24},{40,32},{48,40},{56,48},{64,56},{72,6... | collective-permute-start | bytes 49160 | tf_op jit(solution)/shard_map/ppermute | solution.py:21
  15.5 49.9 %collective-permute-start.21 = (f32[1,32,128]{2,1,0:T(8,128)S(1)}, f32[1,32,128]{2,1,0:T(8,128)S(1)}, u32[]{:S(2)}, u32[]{:S(2)}) collective-permute-start(f32[1,32,128]{2,1,0:T(8,128)S(1)} %get-tuple-element.83), channel_id=1, source_target_pairs={{0,8},{8,16},{16,24},{24,32},{32,40},{40,48},{48,56},{56,64},{64,7... | collective-permute-start | bytes 49160 | tf_op jit(solution)/shard_map/ppermute | solution.py:18
  19.0 84.0 %copy-start.7 = (f32[8,32,128]{2,1,0:T(8,128)}, f32[8,32,128]{2,1,0:T(8,128)S(1)}, u32[]{:S(2)}) copy-start(f32[8,32,128]{2,1,0:T(8,128)S(1)} %get-tuple-element.61) | copy-start | bytes 393220
  19.0 84.0 %copy-start.9 = (f32[8,32,128]{2,1,0:T(8,128)}, f32[8,32,128]{2,1,0:T(8,128)S(1)}, u32[]{:S(2)}) copy-start(f32[8,32,128]{2,1,0:T(8,128)S(1)} %get-tuple-element.62) | copy-start | bytes 393220
  19.0 84.0 %copy-start.11 = (f32[8,32,128]{2,1,0:T(8,128)}, f32[8,32,128]{2,1,0:T(8,128)S(1)}, u32[]{:S(2)}) copy-start(f32[8,32,128]{2,1,0:T(8,128)S(1)} %get-tuple-element.63) | copy-start | bytes 393220
  47.4 39.9 %collective-permute-start.20 = (f32[1,32,128]{2,1,0:T(8,128)S(1)}, f32[1,32,128]{2,1,0:T(8,128)S(1)}, u32[]{:S(2)}, u32[]{:S(2)}) collective-permute-start(f32[1,32,128]{2,1,0:T(8,128)S(1)} %get-tuple-element.82), channel_id=1, source_target_pairs={{8,0},{16,8},{24,16},{32,24},{40,32},{48,40},{56,48},{64,56},{72,6... | collective-permute-start | bytes 49160 | tf_op jit(solution)/shard_map/ppermute | solution.py:21
  50.0 10.7 %copy-start.14 = (f32[5,8,32,128]{3,2,1,0:T(8,128)S(1)}, f32[5,8,32,128]{3,2,1,0:T(8,128)}, u32[]{:S(2)}) copy-start(f32[5,8,32,128]{3,2,1,0:T(8,128)} %param.17) | copy-start | bytes 1966084
  50.5 5.7 %collective-permute-start.2 = (f32[5,10,1,128]{3,0,2,1:T(8,128)S(1)}, f32[5,10,1,128]{3,0,2,1:T(8,128)S(1)}, u32[]{:S(2)}, u32[]{:S(2)}) collective-permute-start(f32[5,10,1,128]{3,0,2,1:T(8,128)S(1)} %get-tuple-element.49), channel_id=1, source_target_pairs={{1,0},{2,1},{3,2},{4,3},{5,4},{6,5},{7,6},{9,8},{10,9},{11,10},{12... | collective-permute-start | bytes 76808 | tf_op jit(solution)/shard_map/ppermute | solution.py:21
  51.8 8.1 %collective-permute-start.3 = (f32[5,10,1,128]{3,0,2,1:T(8,128)S(1)}, f32[5,10,1,128]{3,0,2,1:T(8,128)S(1)}, u32[]{:S(2)}, u32[]{:S(2)}) collective-permute-start(f32[5,10,1,128]{3,0,2,1:T(8,128)S(1)} %get-tuple-element.48), channel_id=1, source_target_pairs={{0,1},{1,2},{2,3},{3,4},{4,5},{5,6},{6,7},{8,9},{9,10},{10,11},{11... | collective-permute-start | bytes 76808 | tf_op jit(solution)/shard_map/ppermute | solution.py:18
  54.8 52.3 %collective-permute-start.18 = (f32[18,1,128]{2,1,0:T(1,128)S(1)}, f32[18,1,128]{2,1,0:T(1,128)S(1)}, u32[]{:S(2)}, u32[]{:S(2)}) collective-permute-start(f32[18,1,128]{2,1,0:T(1,128)S(1)} %get-tuple-element.71), channel_id=1, source_target_pairs={{1,0},{2,1},{3,2},{4,3},{5,4},{6,5},{7,6},{9,8},{10,9},{11,10},{12... | collective-permute-start | bytes 27656 | tf_op jit(solution)/shard_map/ppermute | solution.py:21
  56.2 54.9 %collective-permute-start.19 = (f32[18,1,128]{2,1,0:T(1,128)S(1)}, f32[18,1,128]{2,1,0:T(1,128)S(1)}, u32[]{:S(2)}, u32[]{:S(2)}) collective-permute-start(f32[18,1,128]{2,1,0:T(1,128)S(1)} %get-tuple-element.70), channel_id=1, source_target_pairs={{0,1},{1,2},{2,3},{3,4},{4,5},{5,6},{6,7},{8,9},{9,10},{10,11},{11... | collective-permute-start | bytes 27656 | tf_op jit(solution)/shard_map/ppermute | solution.py:18
  63.4 7.5 %collective-permute-start.4 = (f32[5,1,32,128]{3,0,2,1:T(8,128)S(1)}, f32[5,1,32,128]{3,0,2,1:T(8,128)S(1)}, u32[]{:S(2)}, u32[]{:S(2)}) collective-permute-start(f32[5,1,32,128]{3,0,2,1:T(8,128)S(1)} %get-tuple-element.57), channel_id=1, source_target_pairs={{8,0},{16,8},{24,16},{32,24},{40,32},{48,40},{56,48},{64,56},{72,6... | collective-permute-start | bytes 245768 | tf_op jit(solution)/shard_map/ppermute | solution.py:21
  65.4 7.5 %collective-permute-start.5 = (f32[5,1,32,128]{3,0,2,1:T(8,128)S(1)}, f32[5,1,32,128]{3,0,2,1:T(8,128)S(1)}, u32[]{:S(2)}, u32[]{:S(2)}) collective-permute-start(f32[5,1,32,128]{3,0,2,1:T(8,128)S(1)} %get-tuple-element.56), channel_id=1, source_target_pairs={{0,8},{8,16},{16,24},{24,32},{32,40},{40,48},{48,56},{56,64},{64,7... | collective-permute-start | bytes 245768 | tf_op jit(solution)/shard_map/ppermute | solution.py:18
  72.9 4.4 %collective-permute-start.6 = (f32[5,10,1,128]{3,0,2,1:T(8,128)S(1)}, f32[5,10,1,128]{3,0,2,1:T(8,128)S(1)}, u32[]{:S(2)}, u32[]{:S(2)}) collective-permute-start(f32[5,10,1,128]{3,0,2,1:T(8,128)S(1)} %get-tuple-element.47), channel_id=1, source_target_pairs={{1,0},{2,1},{3,2},{4,3},{5,4},{6,5},{7,6},{9,8},{10,9},{11,10},{12... | collective-permute-start | bytes 76808 | tf_op jit(solution)/shard_map/ppermute | solution.py:21
  74.2 3.9 %collective-permute-start.7 = (f32[5,10,1,128]{3,0,2,1:T(8,128)S(1)}, f32[5,10,1,128]{3,0,2,1:T(8,128)S(1)}, u32[]{:S(2)}, u32[]{:S(2)}) collective-permute-start(f32[5,10,1,128]{3,0,2,1:T(8,128)S(1)} %get-tuple-element.46), channel_id=1, source_target_pairs={{0,1},{1,2},{2,3},{3,4},{4,5},{5,6},{6,7},{8,9},{9,10},{10,11},{11... | collective-permute-start | bytes 76808 | tf_op jit(solution)/shard_map/ppermute | solution.py:18
  81.2 7.5 %collective-permute-start.8 = (f32[5,1,32,128]{3,0,2,1:T(8,128)S(1)}, f32[5,1,32,128]{3,0,2,1:T(8,128)S(1)}, u32[]{:S(2)}, u32[]{:S(2)}) collective-permute-start(f32[5,1,32,128]{3,0,2,1:T(8,128)S(1)} %get-tuple-element.55), channel_id=1, source_target_pairs={{8,0},{16,8},{24,16},{32,24},{40,32},{48,40},{56,48},{64,56},{72,6... | collective-permute-start | bytes 245768 | tf_op jit(solution)/shard_map/ppermute | solution.py:21
  83.1 7.4 %collective-permute-start.9 = (f32[5,1,32,128]{3,0,2,1:T(8,128)S(1)}, f32[5,1,32,128]{3,0,2,1:T(8,128)S(1)}, u32[]{:S(2)}, u32[]{:S(2)}) collective-permute-start(f32[5,1,32,128]{3,0,2,1:T(8,128)S(1)} %get-tuple-element.54), channel_id=1, source_target_pairs={{0,8},{8,16},{16,24},{24,32},{32,40},{40,48},{48,56},{56,64},{64,7... | collective-permute-start | bytes 245768 | tf_op jit(solution)/shard_map/ppermute | solution.py:18
  90.5 6.0 %collective-permute-start.10 = (f32[5,10,1,128]{3,0,2,1:T(8,128)S(1)}, f32[5,10,1,128]{3,0,2,1:T(8,128)S(1)}, u32[]{:S(2)}, u32[]{:S(2)}) collective-permute-start(f32[5,10,1,128]{3,0,2,1:T(8,128)S(1)} %get-tuple-element.45), channel_id=1, source_target_pairs={{1,0},{2,1},{3,2},{4,3},{5,4},{6,5},{7,6},{9,8},{10,9},{11,10},{12... | collective-permute-start | bytes 76808 | tf_op jit(solution)/shard_map/ppermute | solution.py:21
  91.8 10.4 %collective-permute-start.11 = (f32[5,10,1,128]{3,0,2,1:T(8,128)S(1)}, f32[5,10,1,128]{3,0,2,1:T(8,128)S(1)}, u32[]{:S(2)}, u32[]{:S(2)}) collective-permute-start(f32[5,10,1,128]{3,0,2,1:T(8,128)S(1)} %get-tuple-element.44), channel_id=1, source_target_pairs={{0,1},{1,2},{2,3},{3,4},{4,5},{5,6},{6,7},{8,9},{9,10},{10,11},{11... | collective-permute-start | bytes 76808 | tf_op jit(solution)/shard_map/ppermute | solution.py:18
  95.2 24.1 %collective-permute-start.22 = (f32[18,1,128]{2,1,0:T(1,128)S(1)}, f32[18,1,128]{2,1,0:T(1,128)S(1)}, u32[]{:S(2)}, u32[]{:S(2)}) collective-permute-start(f32[18,1,128]{2,1,0:T(1,128)S(1)} %get-tuple-element.73), channel_id=1, source_target_pairs={{1,0},{2,1},{3,2},{4,3},{5,4},{6,5},{7,6},{9,8},{10,9},{11,10},{12... | collective-permute-start | bytes 27656 | tf_op jit(solution)/shard_map/ppermute | solution.py:21
  96.5 22.8 %collective-permute-start.23 = (f32[18,1,128]{2,1,0:T(1,128)S(1)}, f32[18,1,128]{2,1,0:T(1,128)S(1)}, u32[]{:S(2)}, u32[]{:S(2)}) collective-permute-start(f32[18,1,128]{2,1,0:T(1,128)S(1)} %get-tuple-element.72), channel_id=1, source_target_pairs={{0,1},{1,2},{2,3},{3,4},{4,5},{5,6},{6,7},{8,9},{9,10},{10,11},{11... | collective-permute-start | bytes 27656 | tf_op jit(solution)/shard_map/ppermute | solution.py:18
  105.2 7.2 %collective-permute-start.12 = (f32[5,1,32,128]{3,0,2,1:T(8,128)S(1)}, f32[5,1,32,128]{3,0,2,1:T(8,128)S(1)}, u32[]{:S(2)}, u32[]{:S(2)}) collective-permute-start(f32[5,1,32,128]{3,0,2,1:T(8,128)S(1)} %get-tuple-element.53), channel_id=1, source_target_pairs={{8,0},{16,8},{24,16},{32,24},{40,32},{48,40},{56,48},{64,56},{72,6... | collective-permute-start | bytes 245768 | tf_op jit(solution)/shard_map/ppermute | solution.py:21
  107.2 7.5 %collective-permute-start.13 = (f32[5,1,32,128]{3,0,2,1:T(8,128)S(1)}, f32[5,1,32,128]{3,0,2,1:T(8,128)S(1)}, u32[]{:S(2)}, u32[]{:S(2)}) collective-permute-start(f32[5,1,32,128]{3,0,2,1:T(8,128)S(1)} %get-tuple-element.52), channel_id=1, source_target_pairs={{0,8},{8,16},{16,24},{24,32},{32,40},{40,48},{48,56},{56,64},{64,7... | collective-permute-start | bytes 245768 | tf_op jit(solution)/shard_map/ppermute | solution.py:18
  114.7 6.2 %copy-start.8 = (f32[8,32,128]{2,1,0:T(8,128)S(1)}, f32[8,32,128]{2,1,0:T(8,128)}, u32[]{:S(2)}) copy-start(f32[8,32,128]{2,1,0:T(8,128)} %copy-done.7) | copy-start | bytes 393220
  114.7 6.2 %copy-start.10 = (f32[8,32,128]{2,1,0:T(8,128)S(1)}, f32[8,32,128]{2,1,0:T(8,128)}, u32[]{:S(2)}) copy-start(f32[8,32,128]{2,1,0:T(8,128)} %copy-done.9) | copy-start | bytes 393220
  114.7 6.2 %copy-start.12 = (f32[8,32,128]{2,1,0:T(8,128)S(1)}, f32[8,32,128]{2,1,0:T(8,128)}, u32[]{:S(2)}) copy-start(f32[8,32,128]{2,1,0:T(8,128)} %copy-done.11) | copy-start | bytes 393220
  114.7 4.9 %collective-permute-start.14 = (f32[5,10,1,128]{3,0,2,1:T(8,128)S(1)}, f32[5,10,1,128]{3,0,2,1:T(8,128)S(1)}, u32[]{:S(2)}, u32[]{:S(2)}) collective-permute-start(f32[5,10,1,128]{3,0,2,1:T(8,128)S(1)} %get-tuple-element.43), channel_id=1, source_target_pairs={{1,0},{2,1},{3,2},{4,3},{5,4},{6,5},{7,6},{9,8},{10,9},{11,10},{12... | collective-permute-start | bytes 76808 | tf_op jit(solution)/shard_map/ppermute | solution.py:21
  116.2 3.9 %collective-permute-start.15 = (f32[5,10,1,128]{3,0,2,1:T(8,128)S(1)}, f32[5,10,1,128]{3,0,2,1:T(8,128)S(1)}, u32[]{:S(2)}, u32[]{:S(2)}) collective-permute-start(f32[5,10,1,128]{3,0,2,1:T(8,128)S(1)} %get-tuple-element.42), channel_id=1, source_target_pairs={{0,1},{1,2},{2,3},{3,4},{4,5},{5,6},{6,7},{8,9},{9,10},{10,11},{11... | collective-permute-start | bytes 76808 | tf_op jit(solution)/shard_map/ppermute | solution.py:18
  120.9 2.5 copy-start.13
  121.0 61.6 %copy-start.2 = (f32[16,32,128]{2,1,0:T(8,128)S(1)}, f32[16,32,128]{2,1,0:T(8,128)}, u32[]{:S(2)}) copy-start(f32[16,32,128]{2,1,0:T(8,128)} %param.23) | copy-start | bytes 786436
  184.0 5.9 %collective-permute-start.24 = (f32[1,32,128]{2,1,0:T(8,128)S(1)}, f32[1,32,128]{2,1,0:T(8,128)S(1)}, u32[]{:S(2)}, u32[]{:S(2)}) collective-permute-start(f32[1,32,128]{2,1,0:T(8,128)S(1)} %get-tuple-element.79), channel_id=1, source_target_pairs={{8,0},{16,8},{24,16},{32,24},{40,32},{48,40},{56,48},{64,56},{72,6... | collective-permute-start | bytes 49160 | tf_op jit(solution)/shard_map/ppermute | solution.py:21
  186.0 5.6 %collective-permute-start.25 = (f32[1,32,128]{2,1,0:T(8,128)S(1)}, f32[1,32,128]{2,1,0:T(8,128)S(1)}, u32[]{:S(2)}, u32[]{:S(2)}) collective-permute-start(f32[1,32,128]{2,1,0:T(8,128)S(1)} %get-tuple-element.78), channel_id=1, source_target_pairs={{0,8},{8,16},{16,24},{24,32},{32,40},{40,48},{48,56},{56,64},{64,7... | collective-permute-start | bytes 49160 | tf_op jit(solution)/shard_map/ppermute | solution.py:18
  191.6 4.3 %collective-permute-start.26 = (f32[18,1,128]{2,1,0:T(1,128)S(1)}, f32[18,1,128]{2,1,0:T(1,128)S(1)}, u32[]{:S(2)}, u32[]{:S(2)}) collective-permute-start(f32[18,1,128]{2,1,0:T(1,128)S(1)} %get-tuple-element.69), channel_id=1, source_target_pairs={{1,0},{2,1},{3,2},{4,3},{5,4},{6,5},{7,6},{9,8},{10,9},{11,10},{12... | collective-permute-start | bytes 27656 | tf_op jit(solution)/shard_map/ppermute | solution.py:21
  192.9 3.9 %collective-permute-start.27 = (f32[18,1,128]{2,1,0:T(1,128)S(1)}, f32[18,1,128]{2,1,0:T(1,128)S(1)}, u32[]{:S(2)}, u32[]{:S(2)}) collective-permute-start(f32[18,1,128]{2,1,0:T(1,128)S(1)} %get-tuple-element.68), channel_id=1, source_target_pairs={{0,1},{1,2},{2,3},{3,4},{4,5},{5,6},{6,7},{8,9},{9,10},{10,11},{11... | collective-permute-start | bytes 27656 | tf_op jit(solution)/shard_map/ppermute | solution.py:18
  197.5 5.9 %collective-permute-start.28 = (f32[1,32,128]{2,1,0:T(8,128)S(1)}, f32[1,32,128]{2,1,0:T(8,128)S(1)}, u32[]{:S(2)}, u32[]{:S(2)}) collective-permute-start(f32[1,32,128]{2,1,0:T(8,128)S(1)} %get-tuple-element.77), channel_id=1, source_target_pairs={{8,0},{16,8},{24,16},{32,24},{40,32},{48,40},{56,48},{64,56},{72,6... | collective-permute-start | bytes 49160 | tf_op jit(solution)/shard_map/ppermute | solution.py:21
  199.4 5.6 %collective-permute-start.29 = (f32[1,32,128]{2,1,0:T(8,128)S(1)}, f32[1,32,128]{2,1,0:T(8,128)S(1)}, u32[]{:S(2)}, u32[]{:S(2)}) collective-permute-start(f32[1,32,128]{2,1,0:T(8,128)S(1)} %get-tuple-element.76), channel_id=1, source_target_pairs={{0,8},{8,16},{16,24},{24,32},{32,40},{40,48},{48,56},{56,64},{64,7... | collective-permute-start | bytes 49160 | tf_op jit(solution)/shard_map/ppermute | solution.py:18
  205.1 6.4 %collective-permute-start.30 = (f32[18,1,128]{2,1,0:T(1,128)S(1)}, f32[18,1,128]{2,1,0:T(1,128)S(1)}, u32[]{:S(2)}, u32[]{:S(2)}) collective-permute-start(f32[18,1,128]{2,1,0:T(1,128)S(1)} %get-tuple-element.67), channel_id=1, source_target_pairs={{1,0},{2,1},{3,2},{4,3},{5,4},{6,5},{7,6},{9,8},{10,9},{11,10},{12... | collective-permute-start | bytes 27656 | tf_op jit(solution)/shard_map/ppermute | solution.py:21
  206.4 5.9 %collective-permute-start.31 = (f32[18,1,128]{2,1,0:T(1,128)S(1)}, f32[18,1,128]{2,1,0:T(1,128)S(1)}, u32[]{:S(2)}, u32[]{:S(2)}) collective-permute-start(f32[18,1,128]{2,1,0:T(1,128)S(1)} %get-tuple-element.66), channel_id=1, source_target_pairs={{0,1},{1,2},{2,3},{3,4},{4,5},{5,6},{6,7},{8,9},{9,10},{10,11},{11... | collective-permute-start | bytes 27656 | tf_op jit(solution)/shard_map/ppermute | solution.py:18
  213.1 6.2 %collective-permute-start.32 = (f32[1,32,128]{2,1,0:T(8,128)S(1)}, f32[1,32,128]{2,1,0:T(8,128)S(1)}, u32[]{:S(2)}, u32[]{:S(2)}) collective-permute-start(f32[1,32,128]{2,1,0:T(8,128)S(1)} %get-tuple-element.75), channel_id=1, source_target_pairs={{8,0},{16,8},{24,16},{32,24},{40,32},{48,40},{56,48},{64,56},{72,6... | collective-permute-start | bytes 49160 | tf_op jit(solution)/shard_map/ppermute | solution.py:21
  215.0 5.6 %collective-permute-start.33 = (f32[1,32,128]{2,1,0:T(8,128)S(1)}, f32[1,32,128]{2,1,0:T(8,128)S(1)}, u32[]{:S(2)}, u32[]{:S(2)}) collective-permute-start(f32[1,32,128]{2,1,0:T(8,128)S(1)} %get-tuple-element.74), channel_id=1, source_target_pairs={{0,8},{8,16},{16,24},{24,32},{32,40},{40,48},{48,56},{56,64},{64,7... | collective-permute-start | bytes 49160 | tf_op jit(solution)/shard_map/ppermute | solution.py:18
  220.7 6.1 %collective-permute-start.34 = (f32[18,1,128]{2,1,0:T(1,128)S(1)}, f32[18,1,128]{2,1,0:T(1,128)S(1)}, u32[]{:S(2)}, u32[]{:S(2)}) collective-permute-start(f32[18,1,128]{2,1,0:T(1,128)S(1)} %get-tuple-element.65), channel_id=1, source_target_pairs={{1,0},{2,1},{3,2},{4,3},{5,4},{6,5},{7,6},{9,8},{10,9},{11,10},{12... | collective-permute-start | bytes 27656 | tf_op jit(solution)/shard_map/ppermute | solution.py:21
  222.0 5.6 %collective-permute-start.35 = (f32[18,1,128]{2,1,0:T(1,128)S(1)}, f32[18,1,128]{2,1,0:T(1,128)S(1)}, u32[]{:S(2)}, u32[]{:S(2)}) collective-permute-start(f32[18,1,128]{2,1,0:T(1,128)S(1)} %get-tuple-element.64), channel_id=1, source_target_pairs={{0,1},{1,2},{2,3},{3,4},{4,5},{5,6},{6,7},{8,9},{9,10},{10,11},{11... | collective-permute-start | bytes 27656 | tf_op jit(solution)/shard_map/ppermute | solution.py:18
  228.9 141.1 %copy-start.19 = (f32[6]{0:T(128)S(1)}, f32[6]{0:T(128)}, u32[]{:S(2)}) copy-start(f32[6]{0:T(128)} %constant.130) | copy-start | bytes 76
  318.9 51.6 %copy-start.6 = (f32[16,32,128]{2,1,0:T(8,128)}, f32[16,32,128]{2,1,0:T(8,128)S(1)}, u32[]{:S(2)}) copy-start(f32[16,32,128]{2,1,0:T(8,128)S(1)} %divide_add_fusion) | copy-start | bytes 786436
where the time goes:
time: 372 us; the launch traced here: 370 us
  blocking collectives  224 us (60%)
  starting transfers between devices  99.9 us (27%)
  waiting for transfers between devices  18.5 us (5%)
  matrix products  10.4 us (3%)
  other arithmetic  8.88 us (2%)
  local copies, waits for them, and re-layouts  6.83 us (2%)
    psum x1, blocking collectives, shards(): lax.psum(jnp.concatenate([fluid_squares, solid_squares]), ('blk', 'span'))  89.1 us
    ppermute x18, starting transfers between devices, padded(): lax.ppermute(lax.slice_in_dim(block, block.shape[dim] - width, None, axis...  69.2 us
    all_gather x1, blocking collectives, shards(): arrived = lax.all_gather(wall_flux, 'blk', axis=0, tiled=True)  59.1 us
    all_gather x1, blocking collectives, shards(): lax.all_gather(interface_heat_level, 'blk', axis=0, tiled=True)  49.3 us
    ppermute x18, starting transfers between devices, padded(): lax.ppermute(lax.slice_in_dim(block, 0, width, axis=dim), axis, backward)  30.7 us
    unnamed x1, blocking collectives  26.2 us
    ppermute x18, waiting for transfers between devices, padded(): lax.ppermute(lax.slice_in_dim(block, block.shape[dim] - width, None, axis...  14.4 us
    dot_general x4, matrix products, fluid_operator(): jnp.einsum('fg,gxyz->fxyz', jacobian, centre, precision=lax.Precision.HIG...  9.52 us
  transfers between devices with their start and end apart: 36, of which 14 were waited for; matrix products, arithmetic and copies ran while one was open for 4% of the time, Pallas kernels for 0%

commit v1 on v0

v1 whole, which is shorter than its diff:
```python
import functools

import jax
import jax.numpy as jnp
from jax import lax
from jax.experimental import pallas as pl
from jax.experimental.pallas import tpu as pltpu
from jax.sharding import PartitionSpec as P

MESH = pl.DeviceIdType.MESH
F32 = jnp.float32
NF = 5
CX = 8
CY = 32
CH = 16
NZ = 128
ROWS = 48
O = 8
W4 = 4
SWEEPS = 4
OMEGA = 0.8


def kernel(
    nb,
    nsp,
    slot,
    fluid_cells,
    solid_cells,
    adj_in,
    src_in,
    vel_in,
    dif,
    jac,
    wall_in,
    tem_in,
    heat_in,
    con_in,
    owner_in,
    target_in,
    adj_out,
    sol_out,
    norm_out,
    adj,
    src,
    vel,
    inv,
    wall,
    fin,
    tem,
    con,
    heat,
    sgz,
    sd2,
    sdi,
    tout,
    r0,
    r0_up,
    kc,
    cgz,
    cd2,
    cdi,
    hc,
    dl,
    dup,
    dlow,
    pmat,
    pmat_t,
    smat,
    smat_t,
    msend,
    mrecv,
    fsend,
    frecv,
    rsend,
    rrecv,
    nsend,
    nrecv,
    lsem,
    osem,
    fs,
    fr,
    ts,
    tr,
    ks,
    kr,
    xs,
    xr,
    as_,
    ar,
):
    ns = nb * slot
    mb = lax.axis_index("blk")
    ms = lax.axis_index("span")
    has_lo_b, has_hi_b = mb > 0, mb < nb - 1
    has_lo_s, has_hi_s = ms > 0, ms < nsp - 1
    lo_b, hi_b = {"blk": mb - 1}, {"blk": mb + 1}
    lo_s, hi_s = {"span": ms - 1}, {"span": ms + 1}
    has = (has_hi_b, has_lo_b, has_hi_s, has_lo_s)
    came = (has_lo_b, has_hi_b, has_lo_s, has_hi_s)
    peer = (hi_b, lo_b, hi_s, lo_s)

    own = pl.ds(O, CY)

    barrier = pltpu.get_barrier_semaphore()

    def far_first(k, n):
        step = (k + 1) // 2
        return n // 2 + jnp.where(lax.rem(k, 2) == 1, step, -step)

    @pl.loop(0, nb - 1)
    def _(k):
        pl.semaphore_signal(
            barrier, inc=1, device_id={"blk": lax.rem(mb + far_first(k, nb), nb)}, device_id_type=MESH
        )

    @pl.loop(1, nsp)
    def _(k):
        pl.semaphore_signal(barrier, inc=1, device_id={"span": lax.rem(ms + k, nsp)}, device_id_type=MESH)

    loads = [
        pltpu.make_async_copy(adj_in, adj.at[0, :, pl.ds(1, CX), own, :], lsem.at[0]),
        pltpu.make_async_copy(vel_in, vel, lsem.at[1]),
        pltpu.make_async_copy(src_in, src, lsem.at[2]),
        pltpu.make_async_copy(con_in, con.at[pl.ds(1, CH), own, :], lsem.at[3]),
        pltpu.make_async_copy(tem_in, tem.at[0, pl.ds(1, CH), own, :], lsem.at[4]),
        pltpu.make_async_copy(heat_in, heat, lsem.at[5]),
        pltpu.make_async_copy(wall_in.at[0], wall, lsem.at[6]),
    ]
    for copy in loads:
        copy.start()

    def zero_halos(cond, put):
        @pl.when(jnp.logical_not(cond))
        def _():
            put()

    def z_lo_b():
        for e in range(SWEEPS):
            adj[e, :, 0, O : O + CY, :] = jnp.zeros((NF, CY, NZ), F32)
            tem[e, 0, O : O + CY, :] = jnp.zeros((CY, NZ), F32)
        con[0, O : O + CY, :] = jnp.zeros((CY, NZ), F32)
        dlow[...] = jnp.zeros_like(dlow)

    def z_hi_b():
        for e in range(SWEEPS):
            adj[e, :, CX + 1, O : O + CY, :] = jnp.zeros((NF, CY, NZ), F32)
            tem[e, CH + 1, O : O + CY, :] = jnp.zeros((CY, NZ), F32)
        con[CH + 1, O : O + CY, :] = jnp.zeros((CY, NZ), F32)
        kc[5:9, O - W4 : O + CY + W4, :] = jnp.zeros((4, CY + 2 * W4, NZ), F32)
        r0_up[...] = jnp.zeros_like(r0_up)

    def z_span(halo, wide):
        def put():
            for e in range(SWEEPS):
                adj[e, :, 1 : CX + 1, halo : halo + 1, :] = jnp.zeros((NF, CX, 1, NZ), F32)
                tem[e, 1 : CH + 1, halo : halo + 1, :] = jnp.zeros((CH, 1, NZ), F32)
            con[1 : CH + 1, wide : wide + W4, :] = jnp.zeros((CH, W4, NZ), F32)
            hc[4, wide : wide + W4, :] = jnp.zeros((W4, NZ), F32)

        return put

    zero_halos(has_lo_b, z_lo_b)
    zero_halos(has_hi_b, z_hi_b)
    zero_halos(has_lo_s, z_span(O - 1, O - W4))
    zero_halos(has_hi_s, z_span(O + CY, O + CY))

    pl.semaphore_wait(barrier, nb - 1 + nsp - 1)

    def fluid_copy(e, d, first=False):
        if d < 2:
            plane = (CX, 1)[d]
            source = adj_in.at[:, plane - 1] if first else adj.at[e, :, plane, own, :]
            dest = adj.at[e, :, (0, CX + 1)[d], own, :]
        else:
            row = (CY - 1, 0)[d - 2]
            source = (
                adj_in.at[:, :, pl.ds(row, 1), :]
                if first
                else adj.at[e, :, pl.ds(1, CX), pl.ds(O + row, 1), :]
            )
            dest = adj.at[e, :, pl.ds(1, CX), pl.ds((O - 1, O + CY)[d - 2], 1), :]
        return pltpu.make_async_remote_copy(
            source, dest, fs.at[e, d], fr.at[e, d], device_id=peer[d], device_id_type=MESH
        )

    def solid_copy(e, d, first=False):
        if d < 2:
            plane = (CH, 1)[d]
            source = tem_in.at[plane - 1] if first else tem.at[e, plane, own, :]
            dest = tem.at[e, (0, CH + 1)[d], own, :]
        else:
            row = (CY - 1, 0)[d - 2]
            source = (
                tem_in.at[:, pl.ds(row, 1), :]
                if first
                else tem.at[e, pl.ds(1, CH), pl.ds(O + row, 1), :]
            )
            dest = tem.at[e, pl.ds(1, CH), pl.ds((O - 1, O + CY)[d - 2], 1), :]
        return pltpu.make_async_remote_copy(
            source, dest, ts.at[e, d], tr.at[e, d], device_id=peer[d], device_id_type=MESH
        )

    def con_copy(d):
        if d < 2:
            source = con_in.at[(CH - 1, 0)[d]]
            dest = con.at[(0, CH + 1)[d], own, :]
        else:
            source = con_in.at[:, pl.ds((CY - W4, 0)[d - 2], W4), :]
            dest = con.at[pl.ds(1, CH), pl.ds((O - W4, O + CY)[d - 2], W4), :]
        return pltpu.make_async_remote_copy(
            source, dest, ks.at[d], kr.at[d], device_id=peer[d], device_id_type=MESH
        )

    wide_rows = pl.ds(O - W4, CY + 2 * W4)
    wide_copy = pltpu.make_async_remote_copy(
        con.at[pl.ds(1, 4), wide_rows, :],
        kc.at[pl.ds(5, 4), wide_rows, :],
        ks.at[4],
        kr.at[4],
        device_id=lo_b,
        device_id_type=MESH,
    )
    r0_copy = pltpu.make_async_remote_copy(
        r0.at[pl.ds(0, 3)], r0_up, ks.at[5], kr.at[5], device_id=lo_b, device_id_type=MESH
    )
    dl_copy = pltpu.make_async_remote_copy(
        dup, dlow, ks.at[6], kr.at[6], device_id=hi_b, device_id_type=MESH
    )

    def edge_copy(d):
        source = hc.at[4, pl.ds((O + CY - W4, O)[d - 2], W4), :]
        dest = hc.at[4, pl.ds((O - W4, O + CY)[d - 2], W4), :]
        return pltpu.make_async_remote_copy(
            source, dest, ks.at[5 + d], kr.at[5 + d], device_id=peer[d], device_id_type=MESH
        )

    def go(cond, copy):
        @pl.when(cond)
        def _():
            copy.start()

    def arrived(cond, copy):
        @pl.when(cond)
        def _():
            copy.wait_recv()

    def left(cond, copy):
        @pl.when(cond)
        def _():
            copy.wait_send()

    def spread(send, recv, sem):
        @pl.loop(0, nb - 1)
        def _(k):
            to = lax.rem(mb + far_first(k, nb), nb)
            pltpu.make_async_remote_copy(
                send.at[pl.ds(to * slot, slot), :],
                recv.at[pl.ds(mb * slot, slot), :],
                as_.at[sem],
                ar.at[sem],
                device_id={"blk": to},
                device_id_type=MESH,
            ).start()

    def spread_waiter(send, recv, sem):
        rows = pl.ds(0, (nb - 1) * slot)
        return pltpu.make_async_remote_copy(
            send.at[rows, :], recv.at[rows, :], as_.at[sem], ar.at[sem], device_id=hi_b, device_id_type=MESH
        )

    for d in range(4):
        go(has[d], fluid_copy(0, d, True))
    for d in range(4):
        go(has[d], con_copy(d))
    for d in range(4):
        go(has[d], solid_copy(0, d, True))

    own_block = pl.ds(mb * slot, slot)
    ow = owner_in[...].astype(F32)
    tg = target_in[...].astype(F32)
    rows2 = lax.broadcasted_iota(jnp.int32, (CY, CY), 0)
    cols2 = lax.broadcasted_iota(jnp.int32, (CY, CY), 1)
    ow_l = jnp.broadcast_to(ow, (CY, CY))
    ow_s = jnp.sum(jnp.where(rows2 == cols2, ow_l, 0.0), axis=1, keepdims=True)
    same = jnp.where(jnp.broadcast_to(ow_s, (CY, CY)) == ow_l, 1.0, 0.0)
    rank_l = jnp.sum(jnp.where(rows2 < cols2, same, 0.0), axis=0, keepdims=True)
    rank_s = jnp.sum(jnp.where(cols2 < rows2, same, 0.0), axis=1, keepdims=True)
    slot_l = ow * float(slot) + rank_l
    slot_s = ow_s * float(slot) + rank_s
    p_rows = lax.broadcasted_iota(jnp.int32, (ns, CY), 0).astype(F32)
    hot = jnp.broadcast_to(slot_l, (ns, CY)) == p_rows
    pmat[...] = jnp.where(hot, 1.0, 0.0)
    p_cols = lax.broadcasted_iota(jnp.int32, (CY, ns), 1).astype(F32)
    pmat_t[...] = jnp.where(jnp.broadcast_to(slot_s, (CY, ns)) == p_cols, 1.0, 0.0)
    meta = jnp.sum(jnp.where(hot, jnp.broadcast_to(tg + 1.0, (ns, CY)), 0.0), axis=1, keepdims=True) - 1.0
    msend[...] = jnp.broadcast_to(meta, (ns, NZ))
    spread(msend, mrecv, 0)
    mrecv[own_block, :] = msend[own_block, :]

    lane = lax.broadcasted_iota(jnp.int32, (CY, NZ), 1)
    first_lane, last_lane = lane == 0, lane == NZ - 1

    loads[1].wait()

    @pl.loop(0, CX)
    def _(x):
        total = vel[0, x] + vel[1, x] + vel[2, x]
        for f in range(NF):
            inv[f, x] = OMEGA / (total + (6.0 * dif[f] + jac[f, f]))

    for k in range(3):
        dl[k] = jnp.zeros((9, ROWS, NZ), F32)
    for p in range(9):
        if p != 4:
            hc[p] = jnp.zeros((ROWS, NZ), F32)
        kc[p, 0 : O - W4, :] = jnp.zeros((O - W4, NZ), F32)
        kc[p, O + CY + W4 : ROWS, :] = jnp.zeros((ROWS - O - CY - W4, NZ), F32)
    hc[4, 0 : O - W4, :] = jnp.zeros((O - W4, NZ), F32)
    hc[4, O + CY + W4 : ROWS, :] = jnp.zeros((ROWS - O - CY - W4, NZ), F32)

    def fluid_plane(e, x):
        centre = [adj[e, f, x, O : O + CY, :] for f in range(NF)]
        u = [vel[i, x - 1] for i in range(3)]
        total = u[0] + u[1] + u[2]
        squares = []
        for f in range(NF):
            c, d = centre[f], dif[f]
            x_next = adj[e, f, x + 1, O : O + CY, :]
            y_next = adj[e, f, x, O + 1 : O + 1 + CY, :]
            z_next = jnp.where(last_lane, 0.0, pltpu.roll(c, NZ - 1, 1))
            back = (
                adj[e, f, x - 1, O : O + CY, :]
                + adj[e, f, x, O - 1 : O - 1 + CY, :]
                + jnp.where(first_lane, 0.0, pltpu.roll(c, 1, 1))
            )
            residual = src[f, x - 1] - (6.0 * d + total) * c + d * back
            residual = residual + (d + u[0]) * x_next + (d + u[1]) * y_next + (d + u[2]) * z_next
            mixing = jac[f, 0] * centre[0]
            for g in range(1, NF):
                mixing = mixing + jac[f, g] * centre[g]
            residual = residual - mixing
            adj[e + 1, f, x, O : O + CY, :] = c + inv[f, x - 1] * residual
            squares.append(residual)
        return squares

    def folded(values):
        return (values * values).reshape(CY // 8, 8, NZ).sum(axis=0)

    def flows2(q, k, gz, i, a, n):
        c, kk = q[i, pl.ds(a, n), :], k[i, pl.ds(a, n), :]
        flow = (kk + k[i + 1, pl.ds(a, n), :]) * q[i + 1, pl.ds(a, n), :]
        flow = flow + (kk + k[i - 1, pl.ds(a, n), :]) * q[i - 1, pl.ds(a, n), :]
        flow = flow + (kk + k[i, pl.ds(a + 1, n), :]) * q[i, pl.ds(a + 1, n), :]
        flow = flow + (kk + k[i, pl.ds(a - 1, n), :]) * q[i, pl.ds(a - 1, n), :]
        flow = flow + gz * pltpu.roll(c, NZ - 1, 1) + pltpu.roll(gz * c, 1, 1)
        return c, flow

    def coefficients(k, i, a, n):
        kk = k[i, pl.ds(a, n), :]
        at = lax.broadcasted_iota(jnp.int32, (n, NZ), 1)
        k_next = jnp.where(at == NZ - 1, 0.0, pltpu.roll(kk, NZ - 1, 1))
        k_back = jnp.where(at == 0, 0.0, pltpu.roll(kk, 1, 1))
        diagonal = 6.0 * kk + k[i + 1, pl.ds(a, n), :] + k[i - 1, pl.ds(a, n), :]
        diagonal = diagonal + k[i, pl.ds(a + 1, n), :] + k[i, pl.ds(a - 1, n), :] + k_next + k_back
        gz = jnp.where(at == NZ - 1, 0.0, kk + k_next)
        return gz, diagonal

    def solid_plane(e, p):
        c, flow = flows2(tem.at[e], con, sgz[p - 1], p, O, CY)
        residual = heat[p - 1] - 0.5 * (sd2[p - 1] * c - flow)
        return residual, c + sdi[p - 1] * residual

    def solid_prepare():
        loads[3].wait()
        for d in range(4):
            arrived(came[d], con_copy(d))

        @pl.loop(1, CH + 1)
        def _(p):
            gz, diagonal = coefficients(con, p, O, CY)
            sgz[p - 1] = gz
            sd2[p - 1] = diagonal
            sdi[p - 1] = (2.0 * OMEGA) / diagonal

    def solid_wait(e):
        for d in range(4):
            arrived(came[d], solid_copy(e, d, e == 0))

    def solid_sweep(e):
        def put(p):
            tem[e + 1, p, O : O + CY, :] = solid_plane(e, p)[1]

        put(1)
        put(CH)
        for d in range(2):
            go(has[d], solid_copy(e + 1, d))

        @pl.loop(2, CH)
        def _(p):
            put(p)

        for d in range(2, 4):
            go(has[d], solid_copy(e + 1, d))

    loads[0].wait()
    loads[2].wait()
    for e in range(SWEEPS - 1):
        for d in range(4):
            arrived(came[d], fluid_copy(e, d, e == 0))

        @pl.loop(0, 2)
        def _(i):
            fluid_plane(e, 1 + i * (CX - 1))

        for d in range(2):
            go(has[d], fluid_copy(e + 1, d))

        @pl.loop(2, CX)
        def _(x):
            fluid_plane(e, x)

        for d in range(2, 4):
            go(has[d], fluid_copy(e + 1, d))
        if e == 0:
            solid_prepare()
            loads[4].wait()
            loads[5].wait()
        if e == SWEEPS - 2:
            go(has_lo_b, wide_copy)
        solid_wait(e)
        solid_sweep(e)

    n40 = CY + 2 * W4
    for p in range(5):
        kc[p, O - W4 : O + CY + W4, :] = con[12 + p, O - W4 : O + CY + W4, :]

    spread_waiter(msend, mrecv, 0).wait_recv()
    hit = jnp.where(
        mrecv[...] == lax.broadcasted_iota(jnp.int32, (ns, NZ), 1).astype(F32), 1.0, 0.0
    )
    smat_t[...] = hit
    smat[...] = jnp.transpose(hit)
    loads[6].wait()

    e = SWEEPS - 1
    for d in range(4):
        arrived(came[d], fluid_copy(e, d))
    squares = [folded(r) for r in fluid_plane(e, 1)]
    flux = wall[...] * adj[SWEEPS, NF - 1, 1, O : O + CY, :]
    fsend[...] = jnp.dot(pmat[...], flux, precision=lax.Precision.HIGHEST, preferred_element_type=F32)
    spread(fsend, frecv, 1)
    frecv[own_block, :] = fsend[own_block, :]

    def more(x, carry):
        return tuple(a + folded(r) for a, r in zip(carry, fluid_plane(e, x)))

    squares = lax.fori_loop(2, CX + 1, more, tuple(squares))
    outs = [
        pltpu.make_async_copy(
            adj.at[SWEEPS, pl.ds(0, NF - 1), pl.ds(1, CX), own, :], adj_out.at[pl.ds(0, NF - 1)], osem.at[0]
        ),
        pltpu.make_async_copy(
            adj.at[SWEEPS, NF - 1, pl.ds(2, CX - 1), own, :], adj_out.at[NF - 1, pl.ds(1, CX - 1)], osem.at[1]
        ),
    ]
    for copy in outs:
        copy.start()

    solid_wait(e)
    zero8 = jnp.zeros((8, NZ), F32)

    def edge(first, count, at):
        def body(i, carry):
            residual, new = solid_plane(e, first + i)
            tout[first + i - 1] = new
            r0[at + i] = residual
            return carry + folded(residual)

        return lax.fori_loop(0, count, body, zero8)

    low_squares = edge(1, 3, 0)
    go(has_lo_b, r0_copy)
    edge(13, 4, 3)

    def middle(p, carry):
        residual, new = solid_plane(e, p)
        tout[p - 1] = new
        return carry + folded(residual)

    solid_squares = lax.fori_loop(4, 13, middle, zero8)
    outs.append(pltpu.make_async_copy(tout.at[pl.ds(3, 9)], sol_out.at[pl.ds(3, 9)], osem.at[2]))
    outs[-1].start()
    solid_squares = solid_squares + jnp.where(has_lo_b, 0.0, low_squares)

    arrived(has_hi_b, wide_copy)
    row = lax.broadcasted_iota(jnp.int32, (n40, NZ), 0) - W4
    inside = (row >= jnp.where(has_lo_s, -3, 0)) & (row <= jnp.where(has_hi_s, CY + 2, CY - 1))

    @pl.loop(1, 8)
    def _(i):
        gz, diagonal = coefficients(kc, i, O - W4, n40)
        ok = inside & ((i < 5) | has_hi_b)
        cgz[i] = gz
        cd2[i] = diagonal
        cdi[i] = jnp.where(ok, (2.0 * OMEGA) / jnp.where(ok, diagonal, 1.0), 0.0)

    lane8 = lax.broadcasted_iota(jnp.int32, (8, NZ), 1)
    row8 = lax.broadcasted_iota(jnp.int32, (8, NZ), 0)
    sums = jnp.zeros((8, NZ), F32)
    for f in range(NF):
        sums = sums + jnp.where(row8 == f, jnp.broadcast_to(jnp.sum(squares[f], axis=0, keepdims=True), (8, NZ)), 0.0)

    spread_waiter(fsend, frecv, 1).wait_recv()
    surface = jnp.dot(smat[0:CY, :], frecv[...], precision=lax.Precision.HIGHEST, preferred_element_type=F32)
    hc[4, O : O + CY, :] = surface
    for d in (2, 3):
        go(has[d], edge_copy(d))
    for d in (2, 3):
        arrived(came[d], edge_copy(d))
    arrived(has_hi_b, r0_copy)

    wide = slice(O - W4, O + CY + W4)
    dl[0, 4, wide, :] = cdi[4] * hc[4, wide, :]
    for k in range(2):

        @pl.loop(3 - k, 6 + k)
        def _(i):
            c, flow = flows2(dl.at[k], kc, cgz[i], i, O - W4, n40)
            dl[k + 1, i, wide, :] = c + cdi[i] * (hc[i, wide, :] - 0.5 * (cd2[i] * c - flow))

    mid = pl.ds(W4, CY)

    def last(i):
        c, flow = flows2(dl.at[2], kc, cgz[i, mid, :], i, O, CY)
        residual = hc[i, O : O + CY, :] - 0.5 * (cd2[i, mid, :] * c - flow)
        return residual, c + cdi[i, mid, :] * residual

    def last_own(i, carry):
        residual, delta = last(i)
        tout[11 + i] = tout[11 + i] + delta
        return carry + folded(residual + r0[2 + i])

    solid_squares = lax.fori_loop(1, 5, last_own, solid_squares)

    def last_up(i, carry):
        residual, delta = last(i)
        dup[i - 5] = delta
        return carry + folded(residual + r0_up[i - 5])

    up_squares = lax.fori_loop(5, 8, last_up, zero8)
    go(has_hi_b, dl_copy)
    solid_squares = solid_squares + jnp.where(has_hi_b, up_squares, 0.0)
    sums = sums + jnp.where(row8 == NF, jnp.broadcast_to(jnp.sum(solid_squares, axis=0, keepdims=True), (8, NZ)), 0.0)
    totals = jnp.broadcast_to(jnp.sum(sums, axis=1, keepdims=True), (8, NZ))
    totals = jnp.sum(jnp.where(row8 == lane8, totals, 0.0), axis=0, keepdims=True)

    back = jnp.dot(smat_t[:, 0:CY], tout[CH - 1], precision=lax.Precision.HIGHEST, preferred_element_type=F32)
    free = lax.rem(lax.broadcasted_iota(jnp.int32, (ns, NZ), 0), slot) == slot - 1
    rsend[...] = jnp.where(free, jnp.broadcast_to(totals, (ns, NZ)), back)
    spread(rsend, rrecv, 2)
    rrecv[own_block, :] = rsend[own_block, :]
    outs.append(pltpu.make_async_copy(tout.at[pl.ds(12, 4)], sol_out.at[pl.ds(12, 4)], osem.at[3]))
    outs[-1].start()

    arrived(has_lo_b, dl_copy)
    for i in range(3):
        tout[i] = tout[i] + dlow[i]
    outs.append(pltpu.make_async_copy(tout.at[pl.ds(0, 3)], sol_out.at[pl.ds(0, 3)], osem.at[4]))
    outs[-1].start()

    spread_waiter(rsend, rrecv, 2).wait_recv()
    got = rrecv[...]
    nsend[...] = jnp.sum(jnp.where(free, got, 0.0), axis=0, keepdims=True)

    def norm_copy(to):
        return pltpu.make_async_remote_copy(
            nsend, nrecv.at[ms], as_.at[3], ar.at[3], device_id={"span": to}, device_id_type=MESH
        )

    @pl.loop(1, nsp)
    def _(k):
        norm_copy(lax.rem(ms + k, nsp)).start()

    nrecv[ms] = nsend[...]
    returned = jnp.dot(pmat_t[...], got, precision=lax.Precision.HIGHEST, preferred_element_type=F32)
    fin[...] = adj[SWEEPS, NF - 1, 1, O : O + CY, :] + wall[...] * returned
    outs.append(pltpu.make_async_copy(fin, adj_out.at[NF - 1, 0], osem.at[5]))
    outs[-1].start()

    norm_waiter = pltpu.make_async_remote_copy(
        nrecv.at[pl.ds(0, nsp - 1)],
        nrecv.at[pl.ds(0, nsp - 1)],
        as_.at[3],
        ar.at[3],
        device_id=hi_s,
        device_id_type=MESH,
    )
    norm_waiter.wait_recv()
    total = nrecv[0]
    for k in range(1, nsp):
        total = total + nrecv[k]
    cells = jnp.where(lane8 < NF, fluid_cells, solid_cells)
    norm_out[...] = jnp.sqrt(jnp.broadcast_to(total, (8, NZ)) / cells)

    for e in range(SWEEPS):
        for d in range(4):
            left(has[d], fluid_copy(e, d, e == 0))
            left(has[d], solid_copy(e, d, e == 0))
    for d in range(4):
        left(has[d], con_copy(d))
    left(has_lo_b, wide_copy)
    left(has_lo_b, r0_copy)
    left(has_hi_b, dl_copy)
    for d in (2, 3):
        left(has[d], edge_copy(d))
    spread_waiter(msend, mrecv, 0).wait_send()
    spread_waiter(fsend, frecv, 1).wait_send()
    spread_waiter(rsend, rrecv, 2).wait_send()
    norm_waiter.wait_send()
    for copy in outs:
        copy.wait()


def shards(
    nb,
    nsp,
    slot,
    fluid_adjoint_in,
    fluid_source,
    velocity,
    diffusion,
    jacobian,
    wall_coefficient,
    metal_costate_prior,
    solid_source,
    conductivity,
    tile_owner,
    tile_target,
):
    ns = nb * slot
    every = nb * nsp
    anywhere = pl.BlockSpec(memory_space=pl.ANY)
    vmem = pl.BlockSpec(memory_space=pltpu.VMEM)
    smem = pl.BlockSpec(memory_space=pltpu.SMEM)
    V = pltpu.VMEM
    n40 = CY + 2 * W4
    dma = pltpu.SemaphoreType.DMA
    scratch = [
        V((SWEEPS + 1, NF, CX + 2, ROWS, NZ), F32),
        V((NF, CX, CY, NZ), F32),
        V((3, CX, CY, NZ), F32),
        V((NF, CX, CY, NZ), F32),
        V((CY, NZ), F32),
        V((CY, NZ), F32),
        V((SWEEPS, CH + 2, ROWS, NZ), F32),
        V((CH + 2, ROWS, NZ), F32),
        V((CH, CY, NZ), F32),
        V((CH, CY, NZ), F32),
        V((CH, CY, NZ), F32),
        V((CH, CY, NZ), F32),
        V((CH, CY, NZ), F32),
        V((7, CY, NZ), F32),
        V((3, CY, NZ), F32),
        V((9, ROWS, NZ), F32),
        V((8, n40, NZ), F32),
        V((8, n40, NZ), F32),
        V((8, n40, NZ), F32),
        V((9, ROWS, NZ), F32),
        V((3, 9, ROWS, NZ), F32),
        V((3, CY, NZ), F32),
        V((3, CY, NZ), F32),
        V((ns, CY), F32),
        V((CY, ns), F32),
        V((NZ, ns), F32),
        V((ns, NZ), F32),
    ]
    scratch += [V((ns, NZ), F32)] * 6
    scratch += [V((1, NZ), F32), V((nsp, 1, NZ), F32)]
    scratch += [
        dma((7,)),
        dma((6,)),
        dma((SWEEPS, 4)),
        dma((SWEEPS, 4)),
        dma((SWEEPS, 4)),
        dma((SWEEPS, 4)),
        dma((9,)),
        dma((9,)),
        dma((1,)),
        dma((1,)),
        dma((4,)),
        dma((4,)),
    ]
    adjoint, solid, norms = pl.pallas_call(
        functools.partial(
            kernel, nb, nsp, slot, float(CX * CY * NZ * every), float(CH * CY * NZ * every)
        ),
        out_shape=(
            jax.ShapeDtypeStruct(fluid_adjoint_in.shape, F32),
            jax.ShapeDtypeStruct(metal_costate_prior.shape, F32),
            jax.ShapeDtypeStruct((8, NZ), F32),
        ),
        in_specs=[anywhere, anywhere, anywhere, smem, smem, anywhere, anywhere, anywhere, anywhere, vmem, vmem],
        out_specs=(anywhere, anywhere, vmem),
        scratch_shapes=scratch,
        compiler_params=pltpu.CompilerParams(collective_id=0, has_side_effects=True),
        name="iteration",
    )(
        fluid_adjoint_in,
        fluid_source,
        velocity,
        diffusion,
        jacobian,
        wall_coefficient,
        metal_costate_prior,
        solid_source,
        conductivity,
        tile_owner.reshape(1, CY),
        tile_target,
    )
    return adjoint, solid, norms[0, : NF + 1]


def solution(mesh, slot=4):
    placed = (
        P(None, "blk", "span", None),
        P(None, "blk", "span", None),
        P(None, "blk", "span", None),
        P(),
        P(),
        P("blk", "span", None),
        P("blk", "span", None),
        P("blk", "span", None),
        P("blk", "span", None),
        P("span", "blk", None),
        P("span", "blk"),
    )
    return jax.shard_map(
        functools.partial(shards, mesh.shape["blk"], mesh.shape["span"], slot),
        mesh=mesh,
        in_specs=placed,
        out_specs=(P(None, "blk", "span", None), P("blk", "span", None), P()),
        check_vma=False,
    )
```

time: 372 us -> 58 us (0.16)
  the two profiles are of different devices: /device:TPU:2 before, /device:TPU:1 now
where the time goes in v1:
time: 58 us; the launch traced here: 57.8 us
  Pallas kernels  53.2 us (92%)
  local copies, waits for them, and re-layouts  3.92 us (7%)
  between operations  0.64 us (1%)
    pallas_call x1, Pallas kernels, shards(): pl.pallas_call(functools.partial(kernel, nb, nsp, slot, float(CX * CY * N...  53.2 us
    unnamed x4, local copies, waits for them, and re-layouts  2.74 us
    squeeze x1, local copies, waits for them, and re-layouts, shards(): return (adjoint, solid, norms[0, :NF + 1])  1.19 us

profile of v1, /device:TPU:1, one launch (start us, length us, event | category | flops | bytes accessed | tf_op | source)
XLA Modules:
  0.0 57.8 jit_solution(6111324696920175399)
XLA Ops:
  0.6 53.2 %iteration.1 = (f32[5,8,32,128]{3,2,1,0:T(8,128)}, f32[16,32,128]{2,1,0:T(8,128)}, f32[8,128]{1,0:T(8,128)}) custom-call(f32[5,8,32,128]{3,2,1,0:T(8,128)} %adj_in.1, f32[5,8,32,128]{3,2,1,0:T(8,128)} %src_in.1, f32[3,8,32,128]{3,2,1,0:T(8,128)} %vel_in.1, f32[5]{0:T(128)} %dif.1, f32[5,5]{1,0:T(8,128)} %jac.1, f32[1,32,128]{2,1,0:T(8,128)} %wall_in.1, ...), custom_call_target="tpu_custom_call" | custom-call | tf_op jit(solution)/shard_map/iteration/pallas_call | solution.py:694
  53.9 1.2 %slice_bitcast_fusion = f32[6]{0:T(128)} fusion(f32[8,128]{1,0:T(8,128)} %get-tuple-element.8), kind=kLoop, calls=%fused_computation | loop fusion | bytes 48 | tf_op jit(solution)/shard_map/squeeze | solution.py:721
  55.1 0.0 copy-start
  55.1 2.0 %copy.16 = f32[5,8,32,128]{3,2,1,0:T(8,128)} copy(f32[5,8,32,128]{3,2,1,0:T(8,128)} %get-tuple-element.12) | data formatting | bytes 1310720
  57.1 0.0 copy-done
  57.1 0.7 %copy.17 = f32[16,32,128]{2,1,0:T(8,128)} copy(f32[16,32,128]{2,1,0:T(8,128)S(1)} %copy-done) | data formatting | bytes 524288
Async XLA Ops:
  55.1 2.0 %copy-start = (f32[16,32,128]{2,1,0:T(8,128)S(1)}, f32[16,32,128]{2,1,0:T(8,128)}, u32[]{:S(2)}) copy-start(f32[16,32,128]{2,1,0:T(8,128)} %get-tuple-element.13) | copy-start | bytes 786436

commit v2 on v1

--- a/solution.py
+++ b/solution.py
@@ -30,8 +30,8 @@
     adj_in,
     src_in,
     vel_in,
-    dif,
-    jac,
+    dif_in,
+    jac_in,
     wall_in,
     tem_in,
     heat_in,
@@ -41,6 +41,10 @@
     adj_out,
     sol_out,
     norm_out,
+    dif,
+    jac,
+    owner_v,
+    target_v,
     adj,
     src,
     vel,
@@ -88,6 +92,10 @@
     xr,
     as_,
     ar,
+    ws,
+    wr,
+    gb,
+    gs,
 ):
     ns = nb * slot
     mb = lax.axis_index("blk")
@@ -104,19 +112,31 @@
 
     barrier = pltpu.get_barrier_semaphore()
 
+    def around(axis, me, n, distance, sem):
+        for to in (lax.rem(me + distance, n), lax.rem(me + n - distance, n)):
+            pl.semaphore_signal(sem, inc=1, device_id={axis: to}, device_id_type=MESH)
+
+    around("blk", mb, nb, 1, barrier)
+    around("span", ms, nsp, 1, barrier)
+
+    def rounds(n):
+        return max(0, (n // 2 - 1).bit_length())
+
+    def greet(j):
+        if j < rounds(nb):
+            around("blk", mb, nb, 2**j, gb.at[j])
+        if j < rounds(nsp):
+            around("span", ms, nsp, 2**j, gs.at[j])
+
+    def heard(j):
+        if j < rounds(nb):
+            pl.semaphore_wait(gb.at[j], 2)
+        if j < rounds(nsp):
+            pl.semaphore_wait(gs.at[j], 2)
+
     def far_first(k, n):
         step = (k + 1) // 2
         return n // 2 + jnp.where(lax.rem(k, 2) == 1, step, -step)
-
-    @pl.loop(0, nb - 1)
-    def _(k):
-        pl.semaphore_signal(
-            barrier, inc=1, device_id={"blk": lax.rem(mb + far_first(k, nb), nb)}, device_id_type=MESH
-        )
-
-    @pl.loop(1, nsp)
-    def _(k):
-        pl.semaphore_signal(barrier, inc=1, device_id={"span": lax.rem(ms + k, nsp)}, device_id_type=MESH)
 
     loads = [
         pltpu.make_async_copy(adj_in, adj.at[0, :, pl.ds(1, CX), own, :], lsem.at[0]),
@@ -126,6 +146,10 @@
         pltpu.make_async_copy(tem_in, tem.at[0, pl.ds(1, CH), own, :], lsem.at[4]),
         pltpu.make_async_copy(heat_in, heat, lsem.at[5]),
         pltpu.make_async_copy(wall_in.at[0], wall, lsem.at[6]),
+        pltpu.make_async_copy(dif_in, dif, lsem.at[7]),
+        pltpu.make_async_copy(jac_in, jac, lsem.at[8]),
+        pltpu.make_async_copy(owner_in, owner_v, lsem.at[9]),
+        pltpu.make_async_copy(target_in, target_v, lsem.at[10]),
     ]
     for copy in loads:
         copy.start()
@@ -165,23 +189,39 @@
     zero_halos(has_lo_s, z_span(O - 1, O - W4))
     zero_halos(has_hi_s, z_span(O + CY, O + CY))
 
-    pl.semaphore_wait(barrier, nb - 1 + nsp - 1)
+    pl.semaphore_wait(barrier, 4)
+    greet(0)
 
     def fluid_copy(e, d, first=False):
         if d < 2:
             plane = (CX, 1)[d]
-            source = adj_in.at[:, plane - 1] if first else adj.at[e, :, plane, own, :]
-            dest = adj.at[e, :, (0, CX + 1)[d], own, :]
+            fields = pl.ds(0, NF - 1 if (e, d) == (SWEEPS - 1, 0) else NF)
+            source = adj_in.at[:, plane - 1] if first else adj.at[e, fields, plane, own, :]
+            dest = adj.at[e, fields, (0, CX + 1)[d], own, :]
         else:
             row = (CY - 1, 0)[d - 2]
+            planes = pl.ds(2, CX - 1) if e == SWEEPS - 1 else pl.ds(1, CX)
             source = (
                 adj_in.at[:, :, pl.ds(row, 1), :]
                 if first
-                else adj.at[e, :, pl.ds(1, CX), pl.ds(O + row, 1), :]
+                else adj.at[e, :, planes, pl.ds(O + row, 1), :]
             )
-            dest = adj.at[e, :, pl.ds(1, CX), pl.ds((O - 1, O + CY)[d - 2], 1), :]
+            dest = adj.at[e, :, planes, pl.ds((O - 1, O + CY)[d - 2], 1), :]
         return pltpu.make_async_remote_copy(
             source, dest, fs.at[e, d], fr.at[e, d], device_id=peer[d], device_id_type=MESH
+        )
+
+    def early_copy(d):
+        e = SWEEPS - 1
+        if d == 0:
+            source = adj.at[e, NF - 1, CX, own, :]
+            dest = adj.at[e, NF - 1, 0, own, :]
+        else:
+            source = adj.at[e, :, 1, pl.ds(O + (CY - 1, 0)[d - 2], 1), :]
+            dest = adj.at[e, :, 1, pl.ds((O - 1, O + CY)[d - 2], 1), :]
+        i = max(0, d - 1)
+        return pltpu.make_async_remote_copy(
+            source, dest, ws.at[i], wr.at[i], device_id=peer[d], device_id_type=MESH
         )
 
     def solid_copy(e, d, first=False):
@@ -277,8 +317,10 @@
         go(has[d], solid_copy(0, d, True))
 
     own_block = pl.ds(mb * slot, slot)
-    ow = owner_in[...].astype(F32)
-    tg = target_in[...].astype(F32)
+    loads[9].wait()
+    loads[10].wait()
+    ow = owner_v[...].astype(F32)
+    tg = target_v[...].astype(F32)
     rows2 = lax.broadcasted_iota(jnp.int32, (CY, CY), 0)
     cols2 = lax.broadcasted_iota(jnp.int32, (CY, CY), 1)
     ow_l = jnp.broadcast_to(ow, (CY, CY))
@@ -290,18 +332,19 @@
     slot_s = ow_s * float(slot) + rank_s
     p_rows = lax.broadcasted_iota(jnp.int32, (ns, CY), 0).astype(F32)
     hot = jnp.broadcast_to(slot_l, (ns, CY)) == p_rows
-    pmat[...] = jnp.where(hot, 1.0, 0.0)
+    pmat[...] = jnp.where(hot, 1.0, 0.0).astype(jnp.bfloat16)
     p_cols = lax.broadcasted_iota(jnp.int32, (CY, ns), 1).astype(F32)
-    pmat_t[...] = jnp.where(jnp.broadcast_to(slot_s, (CY, ns)) == p_cols, 1.0, 0.0)
+    pmat_t[...] = jnp.where(jnp.broadcast_to(slot_s, (CY, ns)) == p_cols, 1.0, 0.0).astype(jnp.bfloat16)
     meta = jnp.sum(jnp.where(hot, jnp.broadcast_to(tg + 1.0, (ns, CY)), 0.0), axis=1, keepdims=True) - 1.0
     msend[...] = jnp.broadcast_to(meta, (ns, NZ))
-    spread(msend, mrecv, 0)
     mrecv[own_block, :] = msend[own_block, :]
 
     lane = lax.broadcasted_iota(jnp.int32, (CY, NZ), 1)
     first_lane, last_lane = lane == 0, lane == NZ - 1
 
     loads[1].wait()
+    loads[7].wait()
+    loads[8].wait()
 
     @pl.loop(0, CX)
     def _(x):
@@ -319,12 +362,12 @@
     hc[4, 0 : O - W4, :] = jnp.zeros((O - W4, NZ), F32)
     hc[4, O + CY + W4 : ROWS, :] = jnp.zeros((ROWS - O - CY - W4, NZ), F32)
 
-    def fluid_plane(e, x):
+    def fluid_plane(e, x, fields=range(NF)):
         centre = [adj[e, f, x, O : O + CY, :] for f in range(NF)]
         u = [vel[i, x - 1] for i in range(3)]
         total = u[0] + u[1] + u[2]
-        squares = []
-        for f in range(NF):
+        residuals = []
+        for f in fields:
             c, d = centre[f], dif[f]
             x_next = adj[e, f, x + 1, O : O + CY, :]
             y_next = adj[e, f, x, O + 1 : O + 1 + CY, :]
@@ -341,8 +384,17 @@
                 mixing = mixing + jac[f, g] * centre[g]
             residual = residual - mixing
             adj[e + 1, f, x, O : O + CY, :] = c + inv[f, x - 1] * residual
-            squares.append(residual)
-        return squares
+            residuals.append(residual)
+        return residuals
+
+    def select(matrix, values):
+        total = None
+        for _ in range(3):
+            part = values.astype(jnp.bfloat16)
+            values = values - part.astype(F32)
+            term = jnp.dot(matrix, part, preferred_element_type=F32)
+            total = term if total is None else total + term
+        return total
 
     def folded(values):
         return (values * values).reshape(CY // 8, 8, NZ).sum(axis=0)
@@ -408,13 +460,20 @@
     for e in range(SWEEPS - 1):
         for d in range(4):
             arrived(came[d], fluid_copy(e, d, e == 0))
-
-        @pl.loop(0, 2)
-        def _(i):
-            fluid_plane(e, 1 + i * (CX - 1))
-
-        for d in range(2):
-            go(has[d], fluid_copy(e + 1, d))
+        split = e == SWEEPS - 2
+        fluid_plane(e, CX)
+        if split:
+            go(has[0], early_copy(0))
+        go(has[0], fluid_copy(e + 1, 0))
+        fluid_plane(e, 1)
+        if split:
+            for d in (2, 3):
+                go(has[d], early_copy(d))
+        go(has[1], fluid_copy(e + 1, 1))
+
+        if e == 0:
+            heard(0)
+            greet(1)
 
         @pl.loop(2, CX)
         def _(x):
@@ -426,36 +485,43 @@
             solid_prepare()
             loads[4].wait()
             loads[5].wait()
+        if e == 1:
+            heard(2)
+            greet(3)
+        solid_wait(e)
+        solid_sweep(e)
+        if e == 0:
+            heard(1)
+            greet(2)
+        if e == 1:
+            heard(3)
+            spread(msend, mrecv, 0)
         if e == SWEEPS - 2:
             go(has_lo_b, wide_copy)
-        solid_wait(e)
-        solid_sweep(e)
 
     n40 = CY + 2 * W4
     for p in range(5):
         kc[p, O - W4 : O + CY + W4, :] = con[12 + p, O - W4 : O + CY + W4, :]
 
-    spread_waiter(msend, mrecv, 0).wait_recv()
-    hit = jnp.where(
-        mrecv[...] == lax.broadcasted_iota(jnp.int32, (ns, NZ), 1).astype(F32), 1.0, 0.0
-    )
-    smat_t[...] = hit
-    smat[...] = jnp.transpose(hit)
     loads[6].wait()
 
     e = SWEEPS - 1
+    for d in (0, 2, 3):
+        arrived(came[d], early_copy(d))
+    fluid_plane(e, 1, (NF - 1,))
+    flux = wall[...] * adj[SWEEPS, NF - 1, 1, O : O + CY, :]
+    fsend[...] = select(pmat[...], flux)
+    spread(fsend, frecv, 1)
+    frecv[own_block, :] = fsend[own_block, :]
+
     for d in range(4):
         arrived(came[d], fluid_copy(e, d))
-    squares = [folded(r) for r in fluid_plane(e, 1)]
-    flux = wall[...] * adj[SWEEPS, NF - 1, 1, O : O + CY, :]
-    fsend[...] = jnp.dot(pmat[...], flux, precision=lax.Precision.HIGHEST, preferred_element_type=F32)
-    spread(fsend, frecv, 1)
-    frecv[own_block, :] = fsend[own_block, :]
 
     def more(x, carry):
         return tuple(a + folded(r) for a, r in zip(carry, fluid_plane(e, x)))
 
-    squares = lax.fori_loop(2, CX + 1, more, tuple(squares))
+    zero8 = jnp.zeros((8, NZ), F32)
+    squares = lax.fori_loop(1, CX + 1, more, (zero8,) * NF)
     outs = [
         pltpu.make_async_copy(
             adj.at[SWEEPS, pl.ds(0, NF - 1), pl.ds(1, CX), own, :], adj_out.at[pl.ds(0, NF - 1)], osem.at[0]
@@ -468,7 +534,6 @@
         copy.start()
 
     solid_wait(e)
-    zero8 = jnp.zeros((8, NZ), F32)
 
     def edge(first, count, at):
         def body(i, carry):
@@ -511,9 +576,15 @@
     for f in range(NF):
         sums = sums + jnp.where(row8 == f, jnp.broadcast_to(jnp.sum(squares[f], axis=0, keepdims=True), (8, NZ)), 0.0)
 
+    spread_waiter(msend, mrecv, 0).wait_recv()
+    hit = jnp.where(
+        mrecv[...] == lax.broadcasted_iota(jnp.int32, (ns, NZ), 1).astype(F32), 1.0, 0.0
+    )
+    smat_t[...] = hit.astype(jnp.bfloat16)
+    smat[...] = jnp.transpose(hit).astype(jnp.bfloat16)
+
     spread_waiter(fsend, frecv, 1).wait_recv()
-    surface = jnp.dot(smat[0:CY, :], frecv[...], precision=lax.Precision.HIGHEST, preferred_element_type=F32)
-    hc[4, O : O + CY, :] = surface
+    hc[4, O : O + CY, :] = select(smat[0:CY, :], frecv[...])
     for d in (2, 3):
         go(has[d], edge_copy(d))
     for d in (2, 3):
@@ -555,7 +626,7 @@
     totals = jnp.broadcast_to(jnp.sum(sums, axis=1, keepdims=True), (8, NZ))
     totals = jnp.sum(jnp.where(row8 == lane8, totals, 0.0), axis=0, keepdims=True)
 
-    back = jnp.dot(smat_t[:, 0:CY], tout[CH - 1], precision=lax.Precision.HIGHEST, preferred_element_type=F32)
+    back = select(smat_t[:, 0:CY], tout[CH - 1])
     free = lax.rem(lax.broadcasted_iota(jnp.int32, (ns, NZ), 0), slot) == slot - 1
     rsend[...] = jnp.where(free, jnp.broadcast_to(totals, (ns, NZ)), back)
     spread(rsend, rrecv, 2)
@@ -583,7 +654,7 @@
         norm_copy(lax.rem(ms + k, nsp)).start()
 
     nrecv[ms] = nsend[...]
-    returned = jnp.dot(pmat_t[...], got, precision=lax.Precision.HIGHEST, preferred_element_type=F32)
+    returned = select(pmat_t[...], got)
     fin[...] = adj[SWEEPS, NF - 1, 1, O : O + CY, :] + wall[...] * returned
     outs.append(pltpu.make_async_copy(fin, adj_out.at[NF - 1, 0], osem.at[5]))
     outs[-1].start()
@@ -609,6 +680,8 @@
             left(has[d], solid_copy(e, d, e == 0))
     for d in range(4):
         left(has[d], con_copy(d))
+    for d in (0, 2, 3):
+        left(has[d], early_copy(d))
     left(has_lo_b, wide_copy)
     left(has_lo_b, r0_copy)
     left(has_hi_b, dl_copy)
@@ -640,13 +713,20 @@
 ):
     ns = nb * slot
     every = nb * nsp
+
+    def stay(x):
+        return pltpu.with_memory_space_constraint(x, pltpu.HBM)
+
     anywhere = pl.BlockSpec(memory_space=pl.ANY)
     vmem = pl.BlockSpec(memory_space=pltpu.VMEM)
-    smem = pl.BlockSpec(memory_space=pltpu.SMEM)
     V = pltpu.VMEM
     n40 = CY + 2 * W4
     dma = pltpu.SemaphoreType.DMA
     scratch = [
+        pltpu.SMEM((NF,), F32),
+        pltpu.SMEM((NF, NF), F32),
+        V((1, CY), jnp.int32),
+        V((1, CY), jnp.int32),
         V((SWEEPS + 1, NF, CX + 2, ROWS, NZ), F32),
         V((NF, CX, CY, NZ), F32),
         V((3, CX, CY, NZ), F32),
@@ -670,15 +750,15 @@
         V((3, 9, ROWS, NZ), F32),
         V((3, CY, NZ), F32),
         V((3, CY, NZ), F32),
-        V((ns, CY), F32),
-        V((CY, ns), F32),
-        V((NZ, ns), F32),
-        V((ns, NZ), F32),
+        V((ns, CY), jnp.bfloat16),
+        V((CY, ns), jnp.bfloat16),
+        V((NZ, ns), jnp.bfloat16),
+        V((ns, NZ), jnp.bfloat16),
     ]
     scratch += [V((ns, NZ), F32)] * 6
     scratch += [V((1, NZ), F32), V((nsp, 1, NZ), F32)]
     scratch += [
-        dma((7,)),
+        dma((11,)),
         dma((6,)),
         dma((SWEEPS, 4)),
         dma((SWEEPS, 4)),
@@ -690,6 +770,10 @@
         dma((1,)),
         dma((4,)),
         dma((4,)),
+        dma((3,)),
+        dma((3,)),
+        pltpu.SemaphoreType.REGULAR((8,)),
+        pltpu.SemaphoreType.REGULAR((8,)),
     ]
     adjoint, solid, norms = pl.pallas_call(
         functools.partial(
@@ -700,23 +784,28 @@
             jax.ShapeDtypeStruct(metal_costate_prior.shape, F32),
             jax.ShapeDtypeStruct((8, NZ), F32),
         ),
-        in_specs=[anywhere, anywhere, anywhere, smem, smem, anywhere, anywhere, anywhere, anywhere, vmem, vmem],
+        in_specs=[anywhere] * 11,
         out_specs=(anywhere, anywhere, vmem),
         scratch_shapes=scratch,
-        compiler_params=pltpu.CompilerParams(collective_id=0, has_side_effects=True),
+        compiler_params=pltpu.CompilerParams(collective_id=0, has_side_effects=True, vmem_limit_bytes=24 * 2**20),
         name="iteration",
     )(
-        fluid_adjoint_in,
-        fluid_source,
-        velocity,
-        diffusion,
-        jacobian,
-        wall_coefficient,
-        metal_costate_prior,
-        solid_source,
-        conductivity,
-        tile_owner.reshape(1, CY),
-        tile_target,
+        *map(
+            stay,
+            (
+                fluid_adjoint_in,
+                fluid_source,
+                velocity,
+                diffusion,
+                jacobian,
+                wall_coefficient,
+                metal_costate_prior,
+                solid_source,
+                conductivity,
+                tile_owner.reshape(1, CY),
+                tile_target,
+            ),
+        )
     )
     return adjoint, solid, norms[0, : NF + 1]
 

time: 58 us -> 51.3 us (0.88)
  Pallas kernels: 53.2 us -> 48.5 us
  local copies, waits for them, and re-layouts: 3.92 us -> 2.05 us
    pallas_call x1, Pallas kernels: 53.2 us -> 48.5 us  [shards(): pl.pallas_call(functools.partial(kernel, nb, nsp, slot, float(CX * CY * N...]
    unnamed x4 -> x2, local copies, waits for them, and re-layouts: 2.74 us -> 1.54 us
    squeeze x1, local copies, waits for them, and re-layouts: 1.19 us -> 0.51 us  [shards(): return (adjoint, solid, norms[0, :NF + 1])]
where the time goes in v2:
time: 51.3 us; the launch traced here: 51.2 us
  Pallas kernels  48.5 us (95%)
  local copies, waits for them, and re-layouts  2.05 us (4%)
  between operations  0.64 us (1%)
    pallas_call x1, Pallas kernels, shards(): pl.pallas_call(functools.partial(kernel, nb, nsp, slot, float(CX * CY * N...  48.5 us
    unnamed x2, local copies, waits for them, and re-layouts  1.54 us

profile of v2, /device:TPU:1, one launch (start us, length us, event | category | flops | bytes accessed | tf_op | source)
XLA Modules:
  0.0 51.2 jit_solution(15942426415043058167)
XLA Ops:
  0.6 48.5 %iteration.1 = (f32[5,8,32,128]{3,2,1,0:T(8,128)S(1)}, f32[16,32,128]{2,1,0:T(8,128)S(1)}, f32[8,128]{1,0:T(8,128)S(1)}) custom-call(f32[5,8,32,128]{3,2,1,0:T(8,128)} %adj_in.1, f32[5,8,32,128]{3,2,1,0:T(8,128)} %src_in.1, f32[3,8,32,128]{3,2,1,0:T(8,128)} %vel_in.1, f32[5]{0:T(128)} %dif_in.1, f32[5,5]{1,0:T(8,128)} %jac_in.1, f32[1,32,128]{2,1,0:T(8,128)} %wall_in.1, ...), custom_call_target="tpu_custom_call" | custom-call | tf_op jit(solution)/shard_map/iteration/pallas_call | solution.py:778
  49.2 0.5 %slice_bitcast_fusion = f32[6]{0:T(128)} fusion(f32[8,128]{1,0:T(8,128)S(1)} %get-tuple-element.8), kind=kLoop, calls=%fused_computation | loop fusion | bytes 48 | tf_op jit(solution)/shard_map/squeeze | solution.py:810
  49.7 0.8 %copy.16 = f32[5,8,32,128]{3,2,1,0:T(8,128)} copy(f32[5,8,32,128]{3,2,1,0:T(8,128)S(1)} %get-tuple-element.12) | data formatting | bytes 1310720
  50.5 0.7 %copy.17 = f32[16,32,128]{2,1,0:T(8,128)} copy(f32[16,32,128]{2,1,0:T(8,128)S(1)} %get-tuple-element.13) | data formatting | bytes 524288

commit v3 on v2

--- a/solution.py
+++ b/solution.py
@@ -19,6 +19,7 @@
 W4 = 4
 SWEEPS = 4
 OMEGA = 0.8
+GROUPS = ((4, 1), (2, 2), (0, 2))
 
 
 def kernel(
@@ -78,12 +79,17 @@
     frecv,
     rsend,
     rrecv,
+    nmine,
+    nrow,
     nsend,
     nrecv,
     lsem,
     osem,
-    fs,
-    fr,
+    xfs,
+    xfr,
+    yfs,
+    ybr,
+    yir,
     ts,
     tr,
     ks,
@@ -92,8 +98,6 @@
     xr,
     as_,
     ar,
-    ws,
-    wr,
     gb,
     gs,
 ):
@@ -110,6 +114,9 @@
 
     own = pl.ds(O, CY)
 
+    frecv[...] = jnp.zeros_like(frecv)
+    rrecv[...] = jnp.zeros_like(rrecv)
+
     barrier = pltpu.get_barrier_semaphore()
 
     def around(axis, me, n, distance, sem):
@@ -133,10 +140,6 @@
             pl.semaphore_wait(gb.at[j], 2)
         if j < rounds(nsp):
             pl.semaphore_wait(gs.at[j], 2)
-
-    def far_first(k, n):
-        step = (k + 1) // 2
-        return n // 2 + jnp.where(lax.rem(k, 2) == 1, step, -step)
 
     loads = [
         pltpu.make_async_copy(adj_in, adj.at[0, :, pl.ds(1, CX), own, :], lsem.at[0]),
@@ -192,36 +195,43 @@
     pl.semaphore_wait(barrier, 4)
     greet(0)
 
-    def fluid_copy(e, d, first=False):
-        if d < 2:
-            plane = (CX, 1)[d]
-            fields = pl.ds(0, NF - 1 if (e, d) == (SWEEPS - 1, 0) else NF)
-            source = adj_in.at[:, plane - 1] if first else adj.at[e, fields, plane, own, :]
-            dest = adj.at[e, fields, (0, CX + 1)[d], own, :]
-        else:
-            row = (CY - 1, 0)[d - 2]
-            planes = pl.ds(2, CX - 1) if e == SWEEPS - 1 else pl.ds(1, CX)
-            source = (
-                adj_in.at[:, :, pl.ds(row, 1), :]
-                if first
-                else adj.at[e, :, planes, pl.ds(O + row, 1), :]
-            )
-            dest = adj.at[e, :, planes, pl.ds((O - 1, O + CY)[d - 2], 1), :]
+    share = (CX - 2) // len(GROUPS)
+
+    def x_copy(e, d, g):
+        plane, fields = (CX, 1)[d], pl.ds(*GROUPS[g])
         return pltpu.make_async_remote_copy(
-            source, dest, fs.at[e, d], fr.at[e, d], device_id=peer[d], device_id_type=MESH
+            adj_in.at[fields, plane - 1] if e == 0 else adj.at[e, fields, plane, own, :],
+            adj.at[e, fields, (0, CX + 1)[d], own, :],
+            xfs.at[d],
+            xfr.at[e, d, g],
+            device_id=peer[d],
+            device_id_type=MESH,
         )
 
-    def early_copy(d):
-        e = SWEEPS - 1
-        if d == 0:
-            source = adj.at[e, NF - 1, CX, own, :]
-            dest = adj.at[e, NF - 1, 0, own, :]
-        else:
-            source = adj.at[e, :, 1, pl.ds(O + (CY - 1, 0)[d - 2], 1), :]
-            dest = adj.at[e, :, 1, pl.ds((O - 1, O + CY)[d - 2], 1), :]
-        i = max(0, d - 1)
+    def y_copy(e, d, fields, planes, sem):
+        row, halo = (CY - 1, 0)[d - 2], (O - 1, O + CY)[d - 2]
+        inner = pl.ds(planes.start - 1, planes.size)
         return pltpu.make_async_remote_copy(
-            source, dest, ws.at[i], wr.at[i], device_id=peer[d], device_id_type=MESH
+            adj_in.at[fields, inner, pl.ds(row, 1), :]
+            if e == 0
+            else adj.at[e, fields, planes, pl.ds(O + row, 1), :],
+            adj.at[e, fields, planes, pl.ds(halo, 1), :],
+            yfs.at[d - 2],
+            sem,
+            device_id=peer[d],
+            device_id_type=MESH,
+        )
+
+    def outer_copy(e, d, g, x, count=1):
+        return y_copy(e, d, pl.ds(*GROUPS[g]), pl.ds(x, count), ybr.at[e, d - 2, g])
+
+    def inner_copy(e, d, g):
+        return y_copy(e, d, pl.ds(0, NF), pl.ds(2 + share * g, share), yir.at[e, d - 2, g])
+
+    def fluid_sent(d):
+        ref = src.at[:, pl.ds(0, SWEEPS)] if d < 2 else src.at[:, 0]
+        return pltpu.make_async_remote_copy(
+            ref, ref, xfs.at[d] if d < 2 else yfs.at[d - 2], xfr.at[0, 0, 0], device_id=peer[d], device_id_type=MESH
         )
 
     def solid_copy(e, d, first=False):
@@ -290,27 +300,35 @@
         def _():
             copy.wait_send()
 
-    def spread(send, recv, sem):
-        @pl.loop(0, nb - 1)
-        def _(k):
-            to = lax.rem(mb + far_first(k, nb), nb)
+    def spread(send, recv, sem, block, rows):
+        for k in range(nb - 1):
+            step = (k + 1) // 2
+            to = mb + (nb // 2 + (step if k % 2 == 1 else -step))
+            to = jnp.where(to >= nb, to - nb, to)
             pltpu.make_async_remote_copy(
-                send.at[pl.ds(to * slot, slot), :],
-                recv.at[pl.ds(mb * slot, slot), :],
+                send.at[pl.ds(to * block, rows), :] if block else send,
+                recv.at[pl.ds(mb * max(block, rows), rows), :],
                 as_.at[sem],
                 ar.at[sem],
                 device_id={"blk": to},
                 device_id_type=MESH,
             ).start()
 
-    def spread_waiter(send, recv, sem):
-        rows = pl.ds(0, (nb - 1) * slot)
+    def spread_waiter(send, recv, sem, rows):
+        rows = pl.ds(0, (nb - 1) * rows)
         return pltpu.make_async_remote_copy(
-            send.at[rows, :], recv.at[rows, :], as_.at[sem], ar.at[sem], device_id=hi_b, device_id_type=MESH
+            recv.at[rows, :], recv.at[rows, :], as_.at[sem], ar.at[sem], device_id=hi_b, device_id_type=MESH
         )
 
-    for d in range(4):
-        go(has[d], fluid_copy(0, d, True))
+    for g in range(len(GROUPS)):
+        for d in range(2):
+            go(has[d], x_copy(0, d, g))
+        for d in (2, 3):
+            for x in (CX, 1):
+                go(has[d], outer_copy(0, d, g, x))
+    for g in range(len(GROUPS)):
+        for d in (2, 3):
+            go(has[d], inner_copy(0, d, g))
     for d in range(4):
         go(has[d], con_copy(d))
     for d in range(4):
@@ -336,8 +354,16 @@
     p_cols = lax.broadcasted_iota(jnp.int32, (CY, ns), 1).astype(F32)
     pmat_t[...] = jnp.where(jnp.broadcast_to(slot_s, (CY, ns)) == p_cols, 1.0, 0.0).astype(jnp.bfloat16)
     meta = jnp.sum(jnp.where(hot, jnp.broadcast_to(tg + 1.0, (ns, CY)), 0.0), axis=1, keepdims=True) - 1.0
-    msend[...] = jnp.broadcast_to(meta, (ns, NZ))
-    mrecv[own_block, :] = msend[own_block, :]
+    at_row = lax.broadcasted_iota(jnp.int32, (ns, NZ), 0)
+    at_lane = lax.broadcasted_iota(jnp.int32, (ns, NZ), 1)
+    slot_lane = lax.rem(at_row, slot) == at_lane
+    block_of = lax.broadcasted_iota(jnp.int32, (nb, ns), 1) // slot == lax.broadcasted_iota(jnp.int32, (nb, ns), 0)
+    spread_out = jnp.where(slot_lane, jnp.broadcast_to(meta, (ns, NZ)), 0.0).astype(jnp.bfloat16)
+    msend[...] = jnp.dot(
+        jnp.where(block_of, 1.0, 0.0).astype(jnp.bfloat16), spread_out, preferred_element_type=F32
+    )
+    own_row = pl.ds(mb, 1)
+    mrecv[own_row, :] = msend[own_row, :]
 
     lane = lax.broadcasted_iota(jnp.int32, (CY, NZ), 1)
     first_lane, last_lane = lane == 0, lane == NZ - 1
@@ -365,26 +391,28 @@
     def fluid_plane(e, x, fields=range(NF)):
         centre = [adj[e, f, x, O : O + CY, :] for f in range(NF)]
         u = [vel[i, x - 1] for i in range(3)]
-        total = u[0] + u[1] + u[2]
         residuals = []
         for f in fields:
-            c, d = centre[f], dif[f]
+            c = centre[f]
             x_next = adj[e, f, x + 1, O : O + CY, :]
             y_next = adj[e, f, x, O + 1 : O + 1 + CY, :]
             z_next = jnp.where(last_lane, 0.0, pltpu.roll(c, NZ - 1, 1))
-            back = (
-                adj[e, f, x - 1, O : O + CY, :]
-                + adj[e, f, x, O - 1 : O - 1 + CY, :]
-                + jnp.where(first_lane, 0.0, pltpu.roll(c, 1, 1))
+            z_back = jnp.where(first_lane, 0.0, pltpu.roll(c, 1, 1))
+            near = (x_next + adj[e, f, x - 1, O : O + CY, :]) + (y_next + adj[e, f, x, O - 1 : O - 1 + CY, :])
+            near = near + (z_next + z_back)
+            flow = (dif[f] * near + u[0] * x_next) + (u[1] * y_next + u[2] * z_next)
+            others = [g for g in range(NF) if g != f]
+            mixing = (jac[f, others[0]] * centre[others[0]] + jac[f, others[1]] * centre[others[1]]) + (
+                jac[f, others[2]] * centre[others[2]] + jac[f, others[3]] * centre[others[3]]
             )
-            residual = src[f, x - 1] - (6.0 * d + total) * c + d * back
-            residual = residual + (d + u[0]) * x_next + (d + u[1]) * y_next + (d + u[2]) * z_next
-            mixing = jac[f, 0] * centre[0]
-            for g in range(1, NF):
-                mixing = mixing + jac[f, g] * centre[g]
-            residual = residual - mixing
-            adj[e + 1, f, x, O : O + CY, :] = c + inv[f, x - 1] * residual
-            residuals.append(residual)
+            flow = (src[f, x - 1] + flow) - mixing
+            if e == SWEEPS - 1:
+                residual = flow - ((6.0 * dif[f] + jac[f, f]) + (u[0] + u[1] + u[2])) * c
+                new = c + inv[f, x - 1] * residual
+                residuals.append(residual)
+            else:
+                new = (1.0 - OMEGA) * c + inv[f, x - 1] * flow
+            adj[e + 1, f, x, O : O + CY, :] = new
         return residuals
 
     def select(matrix, values):
@@ -420,6 +448,8 @@
 
     def solid_plane(e, p):
         c, flow = flows2(tem.at[e], con, sgz[p - 1], p, O, CY)
+        if e < SWEEPS - 1:
+            return None, (1.0 - OMEGA) * c + sdi[p - 1] * (heat[p - 1] + 0.5 * flow)
         residual = heat[p - 1] - 0.5 * (sd2[p - 1] * c - flow)
         return residual, c + sdi[p - 1] * residual
 
@@ -455,39 +485,44 @@
         for d in range(2, 4):
             go(has[d], solid_copy(e + 1, d))
 
+    def outer_wait(e, g):
+        for d in range(2):
+            arrived(came[d], x_copy(e, d, g))
+        for d in (2, 3):
+            arrived(came[d], outer_copy(e, d, g, 1, 2))
+
+    def inner_wait(e, g):
+        for d in (2, 3):
+            arrived(came[d], inner_copy(e, d, g))
+
     loads[0].wait()
     loads[2].wait()
     for e in range(SWEEPS - 1):
-        for d in range(4):
-            arrived(came[d], fluid_copy(e, d, e == 0))
-        split = e == SWEEPS - 2
-        fluid_plane(e, CX)
-        if split:
-            go(has[0], early_copy(0))
-        go(has[0], fluid_copy(e + 1, 0))
-        fluid_plane(e, 1)
-        if split:
-            for d in (2, 3):
-                go(has[d], early_copy(d))
-        go(has[1], fluid_copy(e + 1, 1))
-
-        if e == 0:
-            heard(0)
-            greet(1)
-
-        @pl.loop(2, CX)
-        def _(x):
-            fluid_plane(e, x)
-
-        for d in range(2, 4):
-            go(has[d], fluid_copy(e + 1, d))
+        for g in range(len(GROUPS)):
+            outer_wait(e, g)
+            for d, x in ((0, CX), (1, 1)):
+                fluid_plane(e, x, range(GROUPS[g][0], sum(GROUPS[g])))
+                go(has[d], x_copy(e + 1, d, g))
+                for k in (2, 3):
+                    go(has[k], outer_copy(e + 1, k, g, x))
+            inner_wait(e, g)
+
+            @pl.loop(2 + share * g, 2 + share * (g + 1))
+            def _(x):
+                fluid_plane(e, x)
+
+            for k in (2, 3):
+                go(has[k], inner_copy(e + 1, k, g))
+            if e == 0 and g == 0:
+                heard(0)
+                greet(1)
+            if e == 1 and g == 0:
+                heard(2)
+                greet(3)
         if e == 0:
             solid_prepare()
             loads[4].wait()
             loads[5].wait()
-        if e == 1:
-            heard(2)
-            greet(3)
         solid_wait(e)
         solid_sweep(e)
         if e == 0:
@@ -495,7 +530,7 @@
             greet(2)
         if e == 1:
             heard(3)
-            spread(msend, mrecv, 0)
+            spread(msend, mrecv, 0, 1, 1)
         if e == SWEEPS - 2:
             go(has_lo_b, wide_copy)
 
@@ -506,16 +541,20 @@
     loads[6].wait()
 
     e = SWEEPS - 1
-    for d in (0, 2, 3):
-        arrived(came[d], early_copy(d))
+    arrived(came[0], x_copy(e, 0, 0))
+    for d in (2, 3):
+        arrived(came[d], outer_copy(e, d, 0, 1, 2))
     fluid_plane(e, 1, (NF - 1,))
     flux = wall[...] * adj[SWEEPS, NF - 1, 1, O : O + CY, :]
     fsend[...] = select(pmat[...], flux)
-    spread(fsend, frecv, 1)
+    spread(fsend, frecv, 1, slot, slot - 1)
     frecv[own_block, :] = fsend[own_block, :]
 
-    for d in range(4):
-        arrived(came[d], fluid_copy(e, d))
+    arrived(came[1], x_copy(e, 1, 0))
+    for g in range(1, len(GROUPS)):
+        outer_wait(e, g)
+    for g in range(len(GROUPS)):
+        inner_wait(e, g)
 
     def more(x, carry):
         return tuple(a + folded(r) for a, r in zip(carry, fluid_plane(e, x)))
@@ -576,14 +615,17 @@
     for f in range(NF):
         sums = sums + jnp.where(row8 == f, jnp.broadcast_to(jnp.sum(squares[f], axis=0, keepdims=True), (8, NZ)), 0.0)
 
-    spread_waiter(msend, mrecv, 0).wait_recv()
-    hit = jnp.where(
-        mrecv[...] == lax.broadcasted_iota(jnp.int32, (ns, NZ), 1).astype(F32), 1.0, 0.0
+    spread_waiter(msend, mrecv, 0, 1).wait_recv()
+    to_slot = lax.broadcasted_iota(jnp.int32, (ns, nb), 0) // slot == lax.broadcasted_iota(jnp.int32, (ns, nb), 1)
+    rows_of = jnp.dot(
+        jnp.where(to_slot, 1.0, 0.0).astype(jnp.bfloat16), mrecv[...].astype(jnp.bfloat16), preferred_element_type=F32
     )
+    rows_of = jnp.sum(jnp.where(slot_lane, rows_of, 0.0), axis=1, keepdims=True)
+    hit = jnp.where(jnp.broadcast_to(rows_of, (ns, NZ)) == at_lane.astype(F32), 1.0, 0.0)
     smat_t[...] = hit.astype(jnp.bfloat16)
     smat[...] = jnp.transpose(hit).astype(jnp.bfloat16)
 
-    spread_waiter(fsend, frecv, 1).wait_recv()
+    spread_waiter(fsend, frecv, 1, slot - 1).wait_recv()
     hc[4, O : O + CY, :] = select(smat[0:CY, :], frecv[...])
     for d in (2, 3):
         go(has[d], edge_copy(d))
@@ -626,10 +668,11 @@
     totals = jnp.broadcast_to(jnp.sum(sums, axis=1, keepdims=True), (8, NZ))
     totals = jnp.sum(jnp.where(row8 == lane8, totals, 0.0), axis=0, keepdims=True)
 
-    back = select(smat_t[:, 0:CY], tout[CH - 1])
-    free = lax.rem(lax.broadcasted_iota(jnp.int32, (ns, NZ), 0), slot) == slot - 1
-    rsend[...] = jnp.where(free, jnp.broadcast_to(totals, (ns, NZ)), back)
-    spread(rsend, rrecv, 2)
+    nmine[...] = totals
+    spread(nmine, nrow, 4, 0, 1)
+    nrow[own_row, :] = totals
+    rsend[...] = select(smat_t[:, 0:CY], tout[CH - 1])
+    spread(rsend, rrecv, 2, slot, slot - 1)
     rrecv[own_block, :] = rsend[own_block, :]
     outs.append(pltpu.make_async_copy(tout.at[pl.ds(12, 4)], sol_out.at[pl.ds(12, 4)], osem.at[3]))
     outs[-1].start()
@@ -640,9 +683,8 @@
     outs.append(pltpu.make_async_copy(tout.at[pl.ds(0, 3)], sol_out.at[pl.ds(0, 3)], osem.at[4]))
     outs[-1].start()
 
-    spread_waiter(rsend, rrecv, 2).wait_recv()
-    got = rrecv[...]
-    nsend[...] = jnp.sum(jnp.where(free, got, 0.0), axis=0, keepdims=True)
+    spread_waiter(nmine, nrow, 4, 1).wait_recv()
+    nsend[...] = jnp.sum(nrow[...], axis=0, keepdims=True)
 
     def norm_copy(to):
         return pltpu.make_async_remote_copy(
@@ -654,7 +696,8 @@
         norm_copy(lax.rem(ms + k, nsp)).start()
 
     nrecv[ms] = nsend[...]
-    returned = select(pmat_t[...], got)
+    spread_waiter(rsend, rrecv, 2, slot - 1).wait_recv()
+    returned = select(pmat_t[...], rrecv[...])
     fin[...] = adj[SWEEPS, NF - 1, 1, O : O + CY, :] + wall[...] * returned
     outs.append(pltpu.make_async_copy(fin, adj_out.at[NF - 1, 0], osem.at[5]))
     outs[-1].start()
@@ -676,22 +719,34 @@
 
     for e in range(SWEEPS):
         for d in range(4):
-            left(has[d], fluid_copy(e, d, e == 0))
             left(has[d], solid_copy(e, d, e == 0))
     for d in range(4):
+        left(has[d], fluid_sent(d))
+    for d in range(4):
         left(has[d], con_copy(d))
-    for d in (0, 2, 3):
-        left(has[d], early_copy(d))
     left(has_lo_b, wide_copy)
     left(has_lo_b, r0_copy)
     left(has_hi_b, dl_copy)
     for d in (2, 3):
         left(has[d], edge_copy(d))
-    spread_waiter(msend, mrecv, 0).wait_send()
-    spread_waiter(fsend, frecv, 1).wait_send()
-    spread_waiter(rsend, rrecv, 2).wait_send()
+    spread_waiter(msend, mrecv, 0, 1).wait_send()
+    spread_waiter(fsend, frecv, 1, slot - 1).wait_send()
+    spread_waiter(rsend, rrecv, 2, slot - 1).wait_send()
+    spread_waiter(nmine, nrow, 4, 1).wait_send()
     norm_waiter.wait_send()
     for copy in outs:
+        copy.wait()
+
+
+def write_kernel(adjoint, solid, norms, adjoint_out, solid_out, norms_out, sem):
+    copies = [
+        pltpu.make_async_copy(adjoint, adjoint_out, sem.at[0]),
+        pltpu.make_async_copy(solid, solid_out, sem.at[1]),
+    ]
+    for copy in copies:
+        copy.start()
+    norms_out[...] = norms[0, 0 : NF + 1]
+    for copy in copies:
         copy.wait()
 
 
@@ -755,23 +810,26 @@
         V((NZ, ns), jnp.bfloat16),
         V((ns, NZ), jnp.bfloat16),
     ]
-    scratch += [V((ns, NZ), F32)] * 6
+    scratch += [V((nb, NZ), F32)] * 2
+    scratch += [V((ns, NZ), F32)] * 4
+    scratch += [V((1, NZ), F32), V((nb, NZ), F32)]
     scratch += [V((1, NZ), F32), V((nsp, 1, NZ), F32)]
     scratch += [
         dma((11,)),
         dma((6,)),
-        dma((SWEEPS, 4)),
-        dma((SWEEPS, 4)),
+        dma((2,)),
+        dma((SWEEPS, 2, len(GROUPS))),
+        dma((2,)),
+        dma((SWEEPS, 2, len(GROUPS))),
+        dma((SWEEPS, 2, len(GROUPS))),
         dma((SWEEPS, 4)),
         dma((SWEEPS, 4)),
         dma((9,)),
         dma((9,)),
         dma((1,)),
         dma((1,)),
-        dma((4,)),
-        dma((4,)),
-        dma((3,)),
-        dma((3,)),
+        dma((5,)),
+        dma((5,)),
         pltpu.SemaphoreType.REGULAR((8,)),
         pltpu.SemaphoreType.REGULAR((8,)),
     ]
@@ -807,7 +865,20 @@
             ),
         )
     )
-    return adjoint, solid, norms[0, : NF + 1]
+    hbm = pl.BlockSpec(memory_space=pltpu.HBM)
+    return pl.pallas_call(
+        write_kernel,
+        out_shape=(
+            jax.ShapeDtypeStruct(fluid_adjoint_in.shape, F32),
+            jax.ShapeDtypeStruct(metal_costate_prior.shape, F32),
+            jax.ShapeDtypeStruct((NF + 1,), F32),
+        ),
+        in_specs=[vmem, vmem, vmem],
+        out_specs=(hbm, hbm, vmem),
+        scratch_shapes=[dma((2,))],
+        compiler_params=pltpu.CompilerParams(vmem_limit_bytes=24 * 2**20),
+        name="write",
+    )(adjoint, solid, norms)
 
 
 def solution(mesh, slot=4):

time: 51.3 us -> 48.6 us (0.947)
  local copies, waits for them, and re-layouts: 2.05 us -> 0 us
  Pallas kernels: 48.5 us -> 47.9 us
    pallas_call x1, Pallas kernels: 48.5 us -> 46.5 us  [shards(): pl.pallas_call(functools.partial(kernel, nb, nsp, slot, float(CX * CY * N...]
    unnamed x2 -> x0, local copies, waits for them, and re-layouts: 1.54 us -> none
    pallas_call x0 -> x1, Pallas kernels: none -> 1.45 us  [shards(): pl.pallas_call(write_kernel, out_shape=(jax.ShapeDtypeStruct(fluid_adjoin...]
    squeeze x1 -> x0, local copies, waits for them, and re-layouts: 0.51 us -> none  [shards(): return (adjoint, solid, norms[0, :NF + 1])]
where the time goes in v3:
time: 48.6 us; the launch traced here: 48.5 us
  Pallas kernels  47.9 us (99%)
  between operations  0.64 us (1%)
    pallas_call x1, Pallas kernels, shards(): pl.pallas_call(functools.partial(kernel, nb, nsp, slot, float(CX * CY * N...  46.5 us
    pallas_call x1, Pallas kernels, shards(): pl.pallas_call(write_kernel, out_shape=(jax.ShapeDtypeStruct(fluid_adjoin...  1.45 us

profile of v3, /device:TPU:1, one launch (start us, length us, event | category | flops | bytes accessed | tf_op | source)
XLA Modules:
  0.0 48.5 jit_solution(12583568088153638830)
XLA Ops:
  0.6 46.5 %iteration.1 = (f32[5,8,32,128]{3,2,1,0:T(8,128)S(1)}, f32[16,32,128]{2,1,0:T(8,128)S(1)}, f32[8,128]{1,0:T(8,128)S(1)}) custom-call(f32[5,8,32,128]{3,2,1,0:T(8,128)} %adj_in.1, f32[5,8,32,128]{3,2,1,0:T(8,128)} %src_in.1, f32[3,8,32,128]{3,2,1,0:T(8,128)} %vel_in.1, f32[5]{0:T(128)} %dif_in.1, f32[5,5]{1,0:T(8,128)} %jac_in.1, f32[1,32,128]{2,1,0:T(8,128)} %wall_in.1, ...), custom_call_target="tpu_custom_call" | custom-call | tf_op jit(solution)/shard_map/iteration/pallas_call | solution.py:836
  47.1 1.4 %write.1 = (f32[5,8,32,128]{3,2,1,0:T(8,128)}, f32[16,32,128]{2,1,0:T(8,128)}, f32[6]{0:T(128)}) custom-call(f32[5,8,32,128]{3,2,1,0:T(8,128)S(1)} %get-tuple-element.6.adjoint, f32[16,32,128]{2,1,0:T(8,128)S(1)} %get-tuple-element.7.solid, f32[8,128]{1,0:T(8,128)S(1)} %get-tuple-element.8.norms), custom_call_target="tpu_custom_call" | custom-call | tf_op jit(solution)/shard_map/write/pallas_call | solution.py:869

commit v4 on v3

--- a/solution.py
+++ b/solution.py
@@ -631,7 +631,6 @@
         go(has[d], edge_copy(d))
     for d in (2, 3):
         arrived(came[d], edge_copy(d))
-    arrived(has_hi_b, r0_copy)
 
     wide = slice(O - W4, O + CY + W4)
     dl[0, 4, wide, :] = cdi[4] * hc[4, wide, :]
@@ -661,6 +660,7 @@
         dup[i - 5] = delta
         return carry + folded(residual + r0_up[i - 5])
 
+    arrived(has_hi_b, r0_copy)
     up_squares = lax.fori_loop(5, 8, last_up, zero8)
     go(has_hi_b, dl_copy)
     solid_squares = solid_squares + jnp.where(has_hi_b, up_squares, 0.0)

time: 48.6 us -> 48.6 us (level)
  no operation moved by 1% of the time
where the time goes in v4:
time: 48.6 us; the launch traced here: 48.5 us
  Pallas kernels  47.9 us (99%)
  between operations  0.64 us (1%)
    pallas_call x1, Pallas kernels, shards(): pl.pallas_call(functools.partial(kernel, nb, nsp, slot, float(CX * CY * N...  46.5 us
    pallas_call x1, Pallas kernels, shards(): pl.pallas_call(write_kernel, out_shape=(jax.ShapeDtypeStruct(fluid_adjoin...  1.45 us

profile of v4, /device:TPU:1, one launch (start us, length us, event | category | flops | bytes accessed | tf_op | source)
XLA Modules:
  0.0 48.5 jit_solution(16685386465746647164)
XLA Ops:
  0.6 46.5 %iteration.1 = (f32[5,8,32,128]{3,2,1,0:T(8,128)S(1)}, f32[16,32,128]{2,1,0:T(8,128)S(1)}, f32[8,128]{1,0:T(8,128)S(1)}) custom-call(f32[5,8,32,128]{3,2,1,0:T(8,128)} %adj_in.1, f32[5,8,32,128]{3,2,1,0:T(8,128)} %src_in.1, f32[3,8,32,128]{3,2,1,0:T(8,128)} %vel_in.1, f32[5]{0:T(128)} %dif_in.1, f32[5,5]{1,0:T(8,128)} %jac_in.1, f32[1,32,128]{2,1,0:T(8,128)} %wall_in.1, ...), custom_call_target="tpu_custom_call" | custom-call | tf_op jit(solution)/shard_map/iteration/pallas_call | solution.py:836
  47.1 1.4 %write.1 = (f32[5,8,32,128]{3,2,1,0:T(8,128)}, f32[16,32,128]{2,1,0:T(8,128)}, f32[6]{0:T(128)}) custom-call(f32[5,8,32,128]{3,2,1,0:T(8,128)S(1)} %get-tuple-element.6.adjoint, f32[16,32,128]{2,1,0:T(8,128)S(1)} %get-tuple-element.7.solid, f32[8,128]{1,0:T(8,128)S(1)} %get-tuple-element.8.norms), custom_call_target="tpu_custom_call" | custom-call | tf_op jit(solution)/shard_map/write/pallas_call | solution.py:869
